TPU v7x, 32 devices: a whole 2x2x4 slice. The times are simulated.
32 devices in a mesh: row: 4 (over y, x), col: 8 (over z, core).
Axes of the slice: x: 2, y: 2, z: 4, core: 2. Of those that a mesh axis runs over, the one named last changes fastest.
Arguments:
- layer_input: bfloat16 [8192, 2048], P(('row', 'col')), may hold values from -6 to 6
- per_layer_input: bfloat16 [8192, 256], P(('row', 'col')), may hold values from -6 to 6
- out_cotangent: bfloat16 [8192, 2048], P(('row', 'col')), may hold values from -6 to 6
- seq_lengths: int32 [4, 3], P('row'), may hold values from 1 to 1024, 2048 in all within a row
- query_weight: bfloat16 [2048, 2048], P('row', 'col'), may hold values from -0.125 to 0.125
- key_weight: bfloat16 [2048, 512], P('row', 'col'), may hold values from -0.125 to 0.125
- value_weight: bfloat16 [2048, 512], P('row', 'col'), may hold values from -0.125 to 0.125
- out_weight: bfloat16 [2048, 2048], P('row', 'col'), may hold values from -0.125 to 0.125
- gate_weight: bfloat16 [2048, 8192], P('row', 'col'), may hold values from -0.125 to 0.125
- up_weight: bfloat16 [2048, 8192], P('row', 'col'), may hold values from -0.125 to 0.125
- down_weight: bfloat16 [2048, 8192], P('row', 'col'), may hold values from -0.0625 to 0.0625
- laurel_down: bfloat16 [2048, 64], P(('row', 'col')), may hold values from -0.125 to 0.125
- laurel_up: bfloat16 [2048, 64], P(('row', 'col')), may hold values from -0.75 to 0.75
- per_layer_gate: bfloat16 [2048, 256], P(('row', 'col')), may hold values from -0.125 to 0.125
- per_layer_projection: bfloat16 [2048, 256], P(('row', 'col')), may hold values from -0.375 to 0.375
- input_gain: bfloat16 [2048], P(('row', 'col')), may hold values from 0.099609375 to 1.8984375
- query_gain: bfloat16 [256], P(('row', 'col')), may hold values from 0.099609375 to 1.8984375
- key_gain: bfloat16 [256], P(('row', 'col')), may hold values from 0.099609375 to 1.8984375
- attention_gain: bfloat16 [2048], P(('row', 'col')), may hold values from 0.099609375 to 1.8984375
- laurel_gain: bfloat16 [2048], P(('row', 'col')), may hold values from 0.099609375 to 1.8984375
- pre_feed_gain: bfloat16 [2048], P(('row', 'col')), may hold values from 0.099609375 to 1.8984375
- post_feed_gain: bfloat16 [2048], P(('row', 'col')), may hold values from 0.099609375 to 1.8984375
- per_layer_gain: bfloat16 [2048], P(('row', 'col')), may hold values from 0.099609375 to 1.8984375
Outputs:
- layer_output: bfloat16 [8192, 2048], P(('row', 'col'))
- input_grad: bfloat16 [8192, 2048], P(('row', 'col'))
- per_layer_grad: bfloat16 [8192, 256], P(('row', 'col'))
- query_weight_grad: float32 [2048, 2048], P('row', 'col')
- key_weight_grad: float32 [2048, 512], P('row', 'col')
- value_weight_grad: float32 [2048, 512], P('row', 'col')
- out_weight_grad: float32 [2048, 2048], P('row', 'col')
- gate_weight_grad: float32 [2048, 8192], P('row', 'col')
- up_weight_grad: float32 [2048, 8192], P('row', 'col')
- down_weight_grad: float32 [2048, 8192], P('row', 'col')
- laurel_down_grad: float32 [2048, 64], P(('row', 'col'))
- laurel_up_grad: float32 [2048, 64], P(('row', 'col'))
- per_layer_gate_grad: float32 [2048, 256], P(('row', 'col'))
- per_layer_projection_grad: float32 [2048, 256], P(('row', 'col'))
- input_gain_grad: float32 [2048], P(('row', 'col'))
- query_gain_grad: float32 [256], P(('row', 'col'))
- key_gain_grad: float32 [256], P(('row', 'col'))
- attention_gain_grad: float32 [2048], P(('row', 'col'))
- laurel_gain_grad: float32 [2048], P(('row', 'col'))
- pre_feed_gain_grad: float32 [2048], P(('row', 'col'))
- post_feed_gain_grad: float32 [2048], P(('row', 'col'))
- per_layer_gain_grad: float32 [2048], P(('row', 'col'))
Inputs may be any that keep to these rules, and one draw needn't show every extreme that they name: `seq_lengths`: row r holds the lengths of the 3 sequences of row group r in token order; they sum to 2048, and the longest is exactly 1024.
All inputs are finite; a program needn't handle non-finite values.
Results may differ from a plain program's by a relative error of at most 0.025.
Values may be sent and summed in bfloat16 or wider, within the bound.
No kernel may reach another device: no remote copies, remote signals or barrier semaphores. Data moves between devices by JAX's collectives and lax.ppermute only.
A program may use at most 320 MiB of HBM per device.

v0:
```python
from functools import partial
import math

import jax
import jax.numpy as jnp
from jax import lax
from jax.sharding import PartitionSpec as P

HEADS = 8
KV_HEADS = 2
HEAD = 256
BLOCK = 256


NORM_EPS = 1e-06
ROOT_HALF = 0.7071067811865476
ROPE_THETA = 1000000.0
NEGATIVE = -1e30


def rms_scale(values, scale_gain):
    return (
        values
        * lax.rsqrt(jnp.mean(values * values, axis=-1, keepdims=True) + NORM_EPS)
        * scale_gain
    )


def rms_plain(values):
    return values * lax.rsqrt(jnp.mean(values * values, axis=-1, keepdims=True) + NORM_EPS)


def rotate(values, position):
    half_width = values.shape[-1] // 2
    steps_up = jnp.arange(half_width, dtype=jnp.float32)
    frequency = jnp.exp(steps_up * (-2.0 * math.log(ROPE_THETA) / values.shape[-1]))
    angle_grid = position.astype(jnp.float32)[:, None] * frequency[None, :]
    cosine = jnp.cos(angle_grid)[:, None, :]
    sine_part = jnp.sin(angle_grid)[:, None, :]
    first_half = values[..., :half_width]
    second_half = values[..., half_width:]
    return jnp.concatenate(
        [
            first_half * cosine - second_half * sine_part,
            second_half * cosine + first_half * sine_part,
        ],
        axis=-1,
    )


def head_prepare(projected, head_gain, position):
    shaped = projected.reshape(projected.shape[0], -1, HEAD)
    return rotate(rms_scale(shaped, head_gain), position)


def placement_info(lengths, token_count):
    finish = jnp.cumsum(lengths)
    begins = finish - lengths
    tokens_at = jnp.arange(token_count, dtype=jnp.int32)
    segment = jnp.sum((tokens_at[:, None] >= finish[None, :]).astype(jnp.int32), axis=1)
    chosen = segment[:, None] == jnp.arange(lengths.shape[0], dtype=jnp.int32)[None, :]
    offset = jnp.sum(jnp.where(chosen, begins[None, :], 0), axis=1)
    return (segment, tokens_at - offset)


def geglu(gate_in, up_in):
    return jax.nn.gelu(gate_in, approximate=True) * up_in


def residual_mix(inputs, attention_out, normed, laurel_out, attention_gain, laurel_gain, pre_gain):
    mixed = (
        inputs
        + rms_scale(attention_out, attention_gain)
        + normed
        + rms_scale(laurel_out, laurel_gain)
    ) * ROOT_HALF
    return (mixed, rms_scale(mixed, pre_gain))


def feed_mix(mixed, down_out, post_gain):
    return mixed + rms_scale(down_out, post_gain)


def final_mix(after_feed, per_out, final_gain):
    return after_feed + rms_scale(per_out, final_gain)


def product(left, right):
    return jnp.dot(left, right, preferred_element_type=jnp.float32)


def product_t(left, right):
    return lax.dot_general(
        left, right, (((1,), (1,)), ((), ())), preferred_element_type=jnp.float32
    )


def product_tn(left, right):
    return lax.dot_general(
        left, right, (((0,), (0,)), ((), ())), preferred_element_type=jnp.float32
    )


def column_inputs(own_rows, weight_cols):
    return product(lax.all_gather(own_rows, "col", axis=0, tiled=True), weight_cols)


def column_input_grad(grad_rows, weight_cols):
    return lax.psum_scatter(
        product_t(grad_rows, weight_cols).astype(jnp.bfloat16),
        "col",
        scatter_dimension=0,
        tiled=True,
    ).astype(jnp.float32)


def column_weight_grad(own_rows, grad_rows):
    return product_tn(lax.all_gather(own_rows, "col", axis=0, tiled=True), grad_rows)


def row_output(hidden_rows, weight_cols):
    return lax.psum_scatter(
        product_t(hidden_rows, weight_cols).astype(jnp.bfloat16),
        "col",
        scatter_dimension=0,
        tiled=True,
    ).astype(jnp.float32)


def row_grads(grad_own, hidden_rows, weight_cols):
    shard_piece = lax.all_gather(grad_own, "col", axis=0, tiled=True)
    weight_total = product_tn(shard_piece, hidden_rows)
    hidden_grad = product(shard_piece, weight_cols)
    return (weight_total, hidden_grad)


def to_heads(token_cols):
    return lax.all_to_all(token_cols, "col", split_axis=0, concat_axis=1, tiled=True)


def to_tokens(head_rows):
    return lax.all_to_all(head_rows, "col", split_axis=1, concat_axis=0, tiled=True)


def local(
    layer_input,
    per_layer_input,
    out_cotangent,
    seq_lengths,
    query_weight,
    key_weight,
    value_weight,
    out_weight,
    gate_weight,
    up_weight,
    down_weight,
    laurel_down,
    laurel_up,
    per_layer_gate,
    per_layer_projection,
    input_gain,
    query_gain,
    key_gain,
    attention_gain,
    laurel_gain,
    pre_feed_gain,
    post_feed_gain,
    per_layer_gain,
):
    row_count = layer_input.shape[0]
    col_count = lax.axis_size("col")
    group_rows = row_count * col_count
    groups = HEADS // KV_HEADS
    score_scale = 1.0 / math.sqrt(HEAD)
    gathered_small = (
        lax.all_gather(laurel_down, ("row", "col"), axis=0, tiled=True),
        lax.all_gather(laurel_up, ("row", "col"), axis=0, tiled=True),
        lax.all_gather(per_layer_gate, ("row", "col"), axis=0, tiled=True),
        lax.all_gather(per_layer_projection, ("row", "col"), axis=0, tiled=True),
        lax.all_gather(input_gain, ("row", "col"), axis=0, tiled=True),
        lax.all_gather(query_gain, ("row", "col"), axis=0, tiled=True),
        lax.all_gather(key_gain, ("row", "col"), axis=0, tiled=True),
        lax.all_gather(attention_gain, ("row", "col"), axis=0, tiled=True),
        lax.all_gather(laurel_gain, ("row", "col"), axis=0, tiled=True),
        lax.all_gather(pre_feed_gain, ("row", "col"), axis=0, tiled=True),
        lax.all_gather(post_feed_gain, ("row", "col"), axis=0, tiled=True),
        lax.all_gather(per_layer_gain, ("row", "col"), axis=0, tiled=True),
    )
    laurel_down_all, laurel_up_all, layer_gate_all, layer_proj_all = (
        gathered_small[0],
        gathered_small[1],
        gathered_small[2],
        gathered_small[3],
    )
    gain_list = [gain_value.astype(jnp.float32) for gain_value in gathered_small[4:]]
    gathered_big = (
        lax.all_gather(query_weight, "row", axis=0, tiled=True),
        lax.all_gather(key_weight, "row", axis=0, tiled=True),
        lax.all_gather(value_weight, "row", axis=0, tiled=True),
        lax.all_gather(out_weight, "row", axis=0, tiled=True),
        lax.all_gather(gate_weight, "row", axis=0, tiled=True),
        lax.all_gather(up_weight, "row", axis=0, tiled=True),
        lax.all_gather(down_weight, "row", axis=0, tiled=True),
    )
    query_cols, key_cols, value_cols, out_cols, gate_cols, up_cols, down_cols = gathered_big
    query_width = query_cols.shape[1]
    kv_width = key_cols.shape[1]
    feed_width = gate_cols.shape[1]
    qkv_cols = jnp.concatenate([query_cols, key_cols, value_cols], axis=1)
    feed_cols = jnp.concatenate([gate_cols, up_cols], axis=1)
    segment, position = placement_info(seq_lengths[0], group_rows)
    own_start = lax.axis_index("col") * row_count
    own_segment = lax.dynamic_slice_in_dim(segment, own_start, row_count, 0)
    own_position = lax.dynamic_slice_in_dim(position, own_start, row_count, 0)
    own_block = own_position // BLOCK
    key_block = position // BLOCK
    block_keys = min(512, group_rows)
    block_count = group_rows // block_keys
    inputs = layer_input.astype(jnp.float32)
    normed, input_pull = jax.vjp(rms_scale, inputs, gain_list[0])
    normed_low = normed.astype(jnp.bfloat16)
    projected = column_inputs(normed_low, qkv_cols).astype(jnp.bfloat16)
    query_part = projected[:, :query_width]
    key_part = projected[:, query_width : query_width + kv_width]
    value_part = projected[:, query_width + kv_width :]
    query_own = to_heads(query_part)
    key_full, value_full = (
        lax.all_gather(key_part, "col", axis=1, tiled=True),
        lax.all_gather(value_part, "col", axis=1, tiled=True),
    )
    query_rot, query_pull = jax.vjp(
        partial(head_prepare, position=own_position), query_own.astype(jnp.float32), gain_list[1]
    )
    key_rot, key_pull = jax.vjp(
        partial(head_prepare, position=position), key_full.astype(jnp.float32), gain_list[2]
    )
    value_normed, value_pull = jax.vjp(
        rms_plain, value_full.astype(jnp.float32).reshape(group_rows, KV_HEADS, HEAD)
    )
    query_low = query_rot.astype(jnp.bfloat16).reshape(row_count, KV_HEADS, groups, HEAD)
    key_low = key_rot.astype(jnp.bfloat16)
    value_heads = value_normed.astype(jnp.bfloat16)

    def key_slice(block_index, source):
        return lax.dynamic_slice_in_dim(source, block_index * block_keys, block_keys, 0)

    def score_block(block_index):
        scores = (
            jnp.einsum(
                "qhgd,khd->hgqk",
                query_low,
                key_slice(block_index, key_low),
                preferred_element_type=jnp.float32,
            )
            * score_scale
        )
        segment_here = key_slice(block_index, segment)
        block_here = key_slice(block_index, key_block)
        allowed = (own_segment[:, None] == segment_here[None, :]) & (
            block_here[None, :] <= own_block[:, None]
        )
        return jnp.where(allowed[None, None], scores, NEGATIVE)

    def stats_step(running, block_index):
        top_seen, total_seen = running
        scores = score_block(block_index)
        new_top = jnp.maximum(top_seen, jnp.max(scores, axis=-1))
        total_seen = total_seen * jnp.exp(top_seen - new_top) + jnp.sum(
            jnp.exp(scores - new_top[..., None]), axis=-1
        )
        return ((new_top, total_seen), None)

    stat_shape = (KV_HEADS, groups, row_count)
    (top_seen, total_seen), unused = lax.scan(
        stats_step,
        (jnp.full(stat_shape, NEGATIVE, jnp.float32), jnp.zeros(stat_shape, jnp.float32)),
        jnp.arange(block_count),
    )
    log_total = top_seen + jnp.log(total_seen)

    def value_step(running, block_index):
        weights = jnp.exp(score_block(block_index) - log_total[..., None]).astype(jnp.bfloat16)
        return (
            running
            + jnp.einsum(
                "hgqk,khd->qhgd",
                weights,
                key_slice(block_index, value_heads),
                preferred_element_type=jnp.float32,
            ),
            None,
        )

    attended, unused = lax.scan(
        value_step,
        jnp.zeros((row_count, KV_HEADS, groups, HEAD), jnp.float32),
        jnp.arange(block_count),
    )
    attended_low = attended.reshape(row_count, HEADS * HEAD).astype(jnp.bfloat16)
    attended_tokens = to_tokens(attended_low)
    attention_out = row_output(attended_tokens, out_cols)
    laurel_mid = product(normed_low, laurel_down_all).astype(jnp.bfloat16)
    laurel_out = product_t(laurel_mid, laurel_up_all)
    (mixed, feed_in), mix_pull = jax.vjp(
        residual_mix,
        inputs,
        attention_out,
        normed_low.astype(jnp.float32),
        laurel_out,
        gain_list[3],
        gain_list[4],
        gain_list[5],
    )
    feed_low = feed_in.astype(jnp.bfloat16)
    gate_up = column_inputs(feed_low, feed_cols)
    hidden, hidden_pull = jax.vjp(geglu, gate_up[:, :feed_width], gate_up[:, feed_width:])
    hidden_low = hidden.astype(jnp.bfloat16)
    down_out = row_output(hidden_low, down_cols)
    after_feed, feed_pull = jax.vjp(feed_mix, mixed, down_out, gain_list[6])
    after_low = after_feed.astype(jnp.bfloat16)
    per_pre = product(after_low, layer_gate_all)
    per_hidden, per_pull = jax.vjp(geglu, per_pre, per_layer_input.astype(jnp.float32))
    per_low = per_hidden.astype(jnp.bfloat16)
    per_out = product_t(per_low, layer_proj_all)
    output, final_pull = jax.vjp(final_mix, after_feed, per_out, gain_list[7])
    after_grad, per_out_grad, final_gain_grad = final_pull(out_cotangent.astype(jnp.float32))
    per_out_low = per_out_grad.astype(jnp.bfloat16)
    per_hidden_grad = product(per_out_low, layer_proj_all)
    layer_proj_grad = product_tn(per_out_low, per_low)
    per_pre_grad, embed_grad = per_pull(per_hidden_grad)
    per_pre_low = per_pre_grad.astype(jnp.bfloat16)
    after_grad = after_grad + product_t(per_pre_low, layer_gate_all)
    layer_gate_grad = product_tn(after_low, per_pre_low)
    mixed_grad, down_grad, post_gain_grad = feed_pull(after_grad)
    down_low = down_grad.astype(jnp.bfloat16)
    down_cols_grad, hidden_grad = row_grads(down_low, hidden_low, down_cols)
    gate_grad, up_grad = hidden_pull(hidden_grad)
    feed_grad_low = jnp.concatenate(
        [gate_grad.astype(jnp.bfloat16), up_grad.astype(jnp.bfloat16)], axis=1
    )
    feed_in_grad = column_input_grad(feed_grad_low, feed_cols)
    feed_cols_grad = column_weight_grad(feed_low, feed_grad_low)
    (
        inputs_grad,
        attention_grad,
        normed_grad,
        laurel_out_grad,
        attention_gain_grad,
        laurel_gain_grad,
        pre_gain_grad,
    ) = mix_pull((mixed_grad, feed_in_grad))
    laurel_out_low = laurel_out_grad.astype(jnp.bfloat16)
    laurel_mid_grad = product(laurel_out_low, laurel_up_all)
    laurel_up_grad = product_tn(laurel_out_low, laurel_mid)
    laurel_mid_low = laurel_mid_grad.astype(jnp.bfloat16)
    normed_grad = normed_grad + product_t(laurel_mid_low, laurel_down_all)
    laurel_down_grad = product_tn(normed_low, laurel_mid_low)
    attention_low = attention_grad.astype(jnp.bfloat16)
    out_cols_grad, attended_tok_grad = row_grads(attention_low, attended_tokens, out_cols)
    attended_grad = to_heads(attended_tok_grad.astype(jnp.bfloat16))
    attended_grad = attended_grad.reshape(row_count, KV_HEADS, groups, HEAD)

    def delta_step(running, block_index):
        probs = jnp.exp(score_block(block_index) - log_total[..., None])
        prob_grad = jnp.einsum(
            "qhgd,khd->hgqk",
            attended_grad,
            key_slice(block_index, value_heads),
            preferred_element_type=jnp.float32,
        )
        return (running + jnp.sum(probs * prob_grad, axis=-1), None)

    delta_sum, unused = lax.scan(
        delta_step, jnp.zeros(stat_shape, jnp.float32), jnp.arange(block_count)
    )

    def grad_step(running, block_index):
        probs = jnp.exp(score_block(block_index) - log_total[..., None])
        prob_grad = jnp.einsum(
            "qhgd,khd->hgqk",
            attended_grad,
            key_slice(block_index, value_heads),
            preferred_element_type=jnp.float32,
        )
        score_grad = (probs * (prob_grad - delta_sum[..., None])).astype(jnp.bfloat16)
        running = (
            running
            + jnp.einsum(
                "hgqk,khd->qhgd",
                score_grad,
                key_slice(block_index, key_low),
                preferred_element_type=jnp.float32,
            )
            * score_scale
        )
        key_part_grad = (
            jnp.einsum("hgqk,qhgd->khd", score_grad, query_low, preferred_element_type=jnp.float32)
            * score_scale
        )
        value_part_grad = jnp.einsum(
            "hgqk,qhgd->khd",
            probs.astype(jnp.bfloat16),
            attended_grad,
            preferred_element_type=jnp.float32,
        )
        return (running, (key_part_grad, value_part_grad))

    query_rot_grad, (key_pieces, value_pieces) = lax.scan(
        grad_step,
        jnp.zeros((row_count, KV_HEADS, groups, HEAD), jnp.float32),
        jnp.arange(block_count),
    )
    query_grad, query_gain_grad = query_pull(query_rot_grad.reshape(row_count, HEADS, HEAD))
    key_grad, key_gain_grad = key_pull(key_pieces.reshape(group_rows, KV_HEADS, HEAD))
    (value_raw_grad,) = value_pull(value_pieces.reshape(group_rows, KV_HEADS, HEAD))
    value_grad = value_raw_grad.reshape(group_rows, KV_HEADS * HEAD)
    key_summed, value_summed = (
        lax.psum_scatter(
            key_grad.astype(jnp.bfloat16), "col", scatter_dimension=1, tiled=True
        ).astype(jnp.float32),
        lax.psum_scatter(
            value_grad.astype(jnp.bfloat16), "col", scatter_dimension=1, tiled=True
        ).astype(jnp.float32),
    )
    query_tok_grad = to_tokens(query_grad.astype(jnp.bfloat16))
    qkv_grad_low = jnp.concatenate(
        [query_tok_grad, key_summed.astype(jnp.bfloat16), value_summed.astype(jnp.bfloat16)], axis=1
    )
    normed_grad = normed_grad + column_input_grad(qkv_grad_low, qkv_cols)
    qkv_cols_grad = column_weight_grad(normed_low, qkv_grad_low)
    input_part, input_gain_grad = input_pull(normed_grad)
    input_total = (inputs_grad + input_part).astype(jnp.bfloat16)
    summed_big = (
        lax.psum_scatter(
            qkv_cols_grad[:, :query_width].astype(jnp.bfloat16),
            "row",
            scatter_dimension=0,
            tiled=True,
        ).astype(jnp.float32),
        lax.psum_scatter(
            qkv_cols_grad[:, query_width : query_width + kv_width].astype(jnp.bfloat16),
            "row",
            scatter_dimension=0,
            tiled=True,
        ).astype(jnp.float32),
        lax.psum_scatter(
            qkv_cols_grad[:, query_width + kv_width :].astype(jnp.bfloat16),
            "row",
            scatter_dimension=0,
            tiled=True,
        ).astype(jnp.float32),
        lax.psum_scatter(
            out_cols_grad.astype(jnp.bfloat16), "row", scatter_dimension=0, tiled=True
        ).astype(jnp.float32),
        lax.psum_scatter(
            feed_cols_grad[:, :feed_width].astype(jnp.bfloat16),
            "row",
            scatter_dimension=0,
            tiled=True,
        ).astype(jnp.float32),
        lax.psum_scatter(
            feed_cols_grad[:, feed_width:].astype(jnp.bfloat16),
            "row",
            scatter_dimension=0,
            tiled=True,
        ).astype(jnp.float32),
        lax.psum_scatter(
            down_cols_grad.astype(jnp.bfloat16), "row", scatter_dimension=0, tiled=True
        ).astype(jnp.float32),
    )
    summed_small = (
        lax.psum_scatter(laurel_down_grad, ("row", "col"), scatter_dimension=0, tiled=True),
        lax.psum_scatter(laurel_up_grad, ("row", "col"), scatter_dimension=0, tiled=True),
        lax.psum_scatter(layer_gate_grad, ("row", "col"), scatter_dimension=0, tiled=True),
        lax.psum_scatter(layer_proj_grad, ("row", "col"), scatter_dimension=0, tiled=True),
        lax.psum_scatter(input_gain_grad, ("row", "col"), scatter_dimension=0, tiled=True),
        lax.psum_scatter(query_gain_grad, ("row", "col"), scatter_dimension=0, tiled=True),
        lax.psum_scatter(key_gain_grad, ("row", "col"), scatter_dimension=0, tiled=True),
        lax.psum_scatter(attention_gain_grad, ("row", "col"), scatter_dimension=0, tiled=True),
        lax.psum_scatter(laurel_gain_grad, ("row", "col"), scatter_dimension=0, tiled=True),
        lax.psum_scatter(pre_gain_grad, ("row", "col"), scatter_dimension=0, tiled=True),
        lax.psum_scatter(post_gain_grad, ("row", "col"), scatter_dimension=0, tiled=True),
        lax.psum_scatter(final_gain_grad, ("row", "col"), scatter_dimension=0, tiled=True),
    )
    return (
        output.astype(jnp.bfloat16),
        input_total,
        embed_grad.astype(jnp.bfloat16),
        summed_big[0],
        summed_big[1],
        summed_big[2],
        summed_big[3],
        summed_big[4],
        summed_big[5],
        summed_big[6],
        summed_small[0],
        summed_small[1],
        summed_small[2],
        summed_small[3],
        summed_small[4],
        summed_small[5],
        summed_small[6],
        summed_small[7],
        summed_small[8],
        summed_small[9],
        summed_small[10],
        summed_small[11],
    )


def solution(mesh):
    in_specs = (
        P(("row", "col"), None),
        P(("row", "col"), None),
        P(("row", "col"), None),
        P("row", None),
        P("row", "col"),
        P("row", "col"),
        P("row", "col"),
        P("row", "col"),
        P("row", "col"),
        P("row", "col"),
        P("row", "col"),
        P(("row", "col"), None),
        P(("row", "col"), None),
        P(("row", "col"), None),
        P(("row", "col"), None),
        P(("row", "col")),
        P(("row", "col")),
        P(("row", "col")),
        P(("row", "col")),
        P(("row", "col")),
        P(("row", "col")),
        P(("row", "col")),
        P(("row", "col")),
    )
    out_specs = (
        P(("row", "col"), None),
        P(("row", "col"), None),
        P(("row", "col"), None),
        P("row", "col"),
        P("row", "col"),
        P("row", "col"),
        P("row", "col"),
        P("row", "col"),
        P("row", "col"),
        P("row", "col"),
        P(("row", "col"), None),
        P(("row", "col"), None),
        P(("row", "col"), None),
        P(("row", "col"), None),
        P(("row", "col")),
        P(("row", "col")),
        P(("row", "col")),
        P(("row", "col")),
        P(("row", "col")),
        P(("row", "col")),
        P(("row", "col")),
        P(("row", "col")),
    )
    return jax.shard_map(local, mesh=mesh, in_specs=in_specs, out_specs=out_specs, check_vma=False)
```

profile of v0, /device:TPU:0, one launch (start us, length us, event | category | flops | bytes accessed | tf_op | source)
XLA Modules:
  0.0 2301.7 jit_solution(12610485705441381439)
XLA Ops:
  15.6 42.6 %all-reduce.21 = (bf16[2048]{0:T(1024)(128)(2,1)S(1)}, bf16[256]{0:T(256)(128)(2,1)S(1)}, bf16[256]{0:T(256)(128)(2,1)S(1)}, bf16[2048]{0:T(1024)(128)(2,1)S(1)}...) all-reduce(bf16[2048]{0:T(1024)(128)(2,1)S(1)} %dynamic-update-slic, ...), channel_id=1, replica_groups=mesh['row'=4,'col'=8] {'row','col'}, use_global_device_ids=true, to_apply=%add.4 | all-reduce | flops 12800 | bytes 51200
  61.2 10.1 all_gather.80
  71.7 8.0 all_gather.81
  80.0 63.2 %all-gather.14.cloned.1.call-done = bf16[2048,2048]{1,0:T(8,128)(2,1)} async-done(((bf16[256,2048]{1,0:T(8,128)(2,1)}), bf16[2048,2048]{1,0:T(8,128)(2,1)}) %all-gather.14.cloned.1.call-update) | async-done | bytes 8388624 | tf_op jit(solution)/shard_map/all_gather | solution.py:105
  143.3 7.1 convolution_convert_fusion.7
  161.2 38.1 %all-to-all-done = bf16[8,256,256]{1,2,0:T(8,128)(2,1)S(1)} async-done(((bf16[8,256,256]{1,2,0:T(8,128)(2,1)}), bf16[8,256,256]{1,2,0:T(8,128)(2,1)S(1)}, u32[]{:S(2)}, u32[]{:S(2)}) %all-to-all-start) | async-done | bytes 1048608 | tf_op jit(solution)/shard_map/all_to_all | solution.py:138
  214.8 30.2 %while.50 = (s32[]{:T(128)}, f32[2,4,256]{2,1,0:T(4,128)S(1)}, f32[2,4,256]{2,1,0:T(4,128)S(1)}, s32[256]{0:T(256)S(1)}, s32[4]{0:T(128)S(1)}, /*index=5*/s32[20...) while((s32[]{:T(128)}, f32[2,4,256]{2,1,0:T(4,128)S(1)}, ...), condition=%wide.region_9.10_spmd.clone, body=%wide.region_6.9_spmd.clone.sunk | while | flops 544614400 | bytes 10475734 | solution.py:274
  258.2 24.9 %while.51 = (s32[]{:T(128)}, f32[256,2,4,256]{0,3,2,1:T(8,128)}, s32[4]{0:T(128)S(1)}, bf16[2048,2,256]{2,0,1:T(8,128)(2,1)}, s32[256]{0:T(256)S(1)}, /*index=5*...) while((s32[]{:T(128)}, f32[256,2,4,256]{0,3,2,1:T(8,128)}, ...), condition=%wide.region_12.13_spmd.clone, body=%wide.region_11.12_spmd.clone.sunk | while | flops 1079377920 | bytes 6577880 | solution.py:294
  293.5 29.6 %all-gather.22.cloned.1.call-done = bf16[2048,256]{1,0:T(8,128)(2,1)} async-done(((bf16[512,256]{1,0:T(8,128)(2,1)}), bf16[2048,256]{1,0:T(8,128)(2,1)}) %all-gather.22.cloned.1.call-update) | async-done | bytes 1048592 | tf_op jit(solution)/shard_map/all_gather | solution.py:200
  323.1 7.3 convolution_convert_fusion.4
  332.1 48.6 %all_gather.88 = bf16[2048,64]{1,0:T(8,128)(2,1)S(1)} all-gather(bf16[64,64]{1,0:T(8,128)(2,1)S(1)} %copy-done.82), channel_id=1, replica_groups=mesh['row'=4,'col'=8] {'row','col'}, dimensions={0}, use_global_device_ids=true | all-gather | bytes 270336 | tf_op jit(solution)/shard_map/all_gather | solution.py:176
  380.7 44.0 %all_gather.89 = bf16[2048,64]{1,0:T(8,128)(2,1)S(1)} all-gather(bf16[64,64]{1,0:T(8,128)(2,1)S(1)} %copy-done.83), channel_id=1, replica_groups=mesh['row'=4,'col'=8] {'row','col'}, dimensions={0}, use_global_device_ids=true | all-gather | bytes 270336 | tf_op jit(solution)/shard_map/all_gather | solution.py:177
  437.2 45.5 %all-gather.26.cloned.1.call-done = bf16[2048,1024]{1,0:T(8,128)(2,1)} async-done(((bf16[512,1024]{1,0:T(8,128)(2,1)}), bf16[2048,1024]{1,0:T(8,128)(2,1)}) %all-gather.26.cloned.1.call-update) | async-done | bytes 4194320 | tf_op jit(solution)/shard_map/all_gather | solution.py:201
  487.3 49.8 %all-gather.28.cloned.1.call-done = bf16[2048,1024]{1,0:T(8,128)(2,1)} async-done(((bf16[512,1024]{1,0:T(8,128)(2,1)}), bf16[2048,1024]{1,0:T(8,128)(2,1)}) %all-gather.28.cloned.1.call-update) | async-done | bytes 4194320 | tf_op jit(solution)/shard_map/all_gather | solution.py:202
  541.7 79.6 %all-gather.24.cloned.1.call-done = bf16[2048,2048]{1,0:T(8,128)(2,1)} async-done(((bf16[256,2048]{1,0:T(8,128)(2,1)}), bf16[2048,2048]{1,0:T(8,128)(2,1)}) %all-gather.24.cloned.1.call-update) | async-done | bytes 8388624 | tf_op jit(solution)/shard_map/all_gather | solution.py:105
  621.3 24.3 %fusion.150 = f32[2048,2048]{0,1:T(8,128)} fusion(bf16[2048,2048]{1,0:T(8,128)(2,1)} %all-gather.24.cloned.1.call-done, bf16[2048,2048]{1,0:T(8,128)(2,1)} %constant_dynamic-update-slice_fusion), kind=kOutput, calls=%fused_computation.286 | convolution fusion | flops 17179869184 | bytes 33554432 | tf_op jit(solution)/shard_map/dot_general | solution.py:89
  645.7 10.1 multiply_convert_fusion.1
  655.8 18.3 all-gather.30.cloned.1.call-done
  674.1 14.1 convolution_convert_fusion.3
  690.3 89.7 %reduce-scatter.22.cloned.1.call-done = bf16[256,2048]{1,0:T(8,128)(2,1)} async-done(((bf16[2048,2048]{1,0:T(8,128)(2,1)}), bf16[256,2048]{1,0:T(8,128)(2,1)}) %reduce-scatter.22.cloned.1.call-update) | async-done | bytes 1048592 | tf_op jit(solution)/shard_map/reduce_scatter | solution.py:122
  783.3 9.5 all-gather.32.cloned.1.call-done
  794.6 54.0 %all-gather.34.cloned.1.call-done = bf16[2048,256]{1,0:T(8,128)(2,1)} async-done(((bf16[64,256]{1,0:T(8,128)(2,1)}), bf16[2048,256]{1,0:T(8,128)(2,1)}) %all-gather.34.cloned.1.call-update) | async-done | bytes 1048592 | tf_op jit(solution)/shard_map/all_gather | solution.py:179
  860.3 81.1 %all-gather.36.cloned.1.call-done = bf16[2048,2048]{1,0:T(8,128)(2,1)} async-done(((bf16[256,2048]{1,0:T(8,128)(2,1)}), bf16[2048,2048]{1,0:T(8,128)(2,1)}) %all-gather.36.cloned.1.call-update) | async-done | bytes 8388624 | tf_op jit(solution)/shard_map/all_gather | solution.py:131
  941.4 24.3 %fusion.67 = (bf16[2048,1024]{0,1:T(8,128)(2,1)}, bf16[2048,1024]{0,1:T(8,128)(2,1)}) fusion(f32[2048,2048]{0,1:T(8,128)} %fusion.150, bf16[2048,2048]{1,0:T(8,128)(2,1)} %all-gather.36.cloned.1.call-done, bf16[2048,1024]{1,0:T(8,128)(2,1)} %all-gather.30.cloned.1.call-done), kind=kOutput, calls=%fused_computation.78 | convolution fusion | flops 8640266240 | bytes 37748736 | tf_op jit(solution)/shard_map/dot_general | solution.py:89
  965.7 24.1 %convolution_convert_fusion.2 = bf16[2048,2048]{1,0:T(8,128)(2,1)} fusion(bf16[2048,2048]{1,0:T(8,128)(2,1)} %constant_dynamic-update-slice_fusion, bf16[2048,1024]{0,1:T(8,128)(2,1)} %get-tuple-element.772, bf16[2048,1024]{0,1:T(8,128)(2,1)} %get-tuple-element.771), kind=kOutput, calls=%fused_computation.85 | convolution fusion | flops 17200840704 | bytes 25165824 | tf_op jit(solution)/shard_map/dot_general | solution.py:93
  990.5 87.5 %reduce-scatter.24.cloned.1.call-done = bf16[256,2048]{1,0:T(8,128)(2,1)} async-done(((bf16[2048,2048]{1,0:T(8,128)(2,1)}), bf16[256,2048]{1,0:T(8,128)(2,1)}) %reduce-scatter.24.cloned.1.call-update) | async-done | bytes 1048592 | tf_op jit(solution)/shard_map/reduce_scatter | solution.py:109
  1087.7 80.6 %all-gather.38.cloned.1.call-done = bf16[2048,2048]{1,0:T(8,128)(2,1)} async-done(((bf16[256,2048]{1,0:T(8,128)(2,1)}), bf16[2048,2048]{1,0:T(8,128)(2,1)}) %all-gather.38.cloned.1.call-update) | async-done | bytes 8388624 | tf_op jit(solution)/shard_map/all_gather | solution.py:131
  1179.6 26.5 %all-to-all-done.2 = bf16[8,256,256]{2,1,0:T(8,128)(2,1)} async-done(((bf16[8,256,256]{2,1,0:T(8,128)(2,1)}), bf16[8,256,256]{2,1,0:T(8,128)(2,1)}, u32[]{:S(2)}, u32[]{:S(2)}) %all-to-all-start.2) | async-done | bytes 1048608 | tf_op jit(solution)/shard_map/all_to_all | solution.py:138
  1206.1 25.0 %while.52 = (s32[]{:T(128)}, f32[2,4,256]{2,1,0:T(4,128)S(1)}, s32[256]{0:T(256)S(1)}, s32[4]{0:T(128)S(1)}, s32[2048]{0:T(1024)S(1)}, /*index=5*/s32[2048]{0:T(...) while((s32[]{:T(128)}, f32[2,4,256]{2,1,0:T(4,128)S(1)}, ...), condition=%wide.region_28.29_spmd.clone, body=%wide.region_26.28_spmd.clone.sunk | while | flops 1079379968 | bytes 11852009 | solution.py:373
  1231.1 55.9 %while.53 = (s32[]{:T(128)}, f32[256,2,4,256]{0,3,2,1:T(8,128)S(1)}, f32[4,512,2,256]{3,1,0,2:T(8,128)}, f32[4,512,2,256]{3,1,2,0:T(8,128)}, s32[4]{0:T(128)S(1)...) while((s32[]{:T(128)}, ...), condition=%wide.region_30.31_spmd.clone, body=%wide.region_29.30_spmd.clone.sunk | while | flops 2697068544 | bytes 39755040 | solution.py:408
  1318.3 14.1 convolution_convert_fusion.5
  1332.4 23.4 %convolution_convert_fusion = bf16[2048,2048]{1,0:T(8,128)(2,1)S(1)} fusion(bf16[2048,2048]{1,0:T(8,128)(2,1)} %all-gather.24.cloned.1.call-done, bf16[2048,1024]{0,1:T(8,128)(2,1)} %get-tuple-element.772, bf16[2048,1024]{0,1:T(8,128)(2,1)} %get-tuple-element.771), kind=kOutput, calls=%fused_computation.83 | convolution fusion | flops 17200840704 | bytes 25165824 | tf_op jit(solution)/shard_map/dot_general | solution.py:99
  1368.1 6.9 convolution_convert_fusion.8
  1375.1 19.4 all-to-all-done.3
  1398.6 7.0 convolution_convert_fusion.6
  1408.5 9.6 convolution_convert_fusion.1
  1430.4 50.6 %reduce-scatter.38.cloned.1.call-done = bf16[512,1024]{1,0:T(8,128)(2,1)} async-done(((bf16[2048,1024]{1,0:T(8,128)(2,1)}), bf16[512,1024]{1,0:T(8,128)(2,1)}) %reduce-scatter.38.cloned.1.call-update) | async-done | bytes 1048592 | tf_op jit(solution)/shard_map/reduce_scatter | solution.py:455
  1483.8 52.8 %reduce-scatter.40.cloned.1.call-done = bf16[512,1024]{1,0:T(8,128)(2,1)} async-done(((bf16[2048,1024]{1,0:T(8,128)(2,1)}), bf16[512,1024]{1,0:T(8,128)(2,1)}) %reduce-scatter.40.cloned.1.call-update) | async-done | bytes 1048592 | tf_op jit(solution)/shard_map/reduce_scatter | solution.py:461
  1541.1 26.3 %reduce-scatter.36.cloned.1.call-done = bf16[512,256]{1,0:T(8,128)(2,1)} async-done(((bf16[2048,256]{1,0:T(8,128)(2,1)}), bf16[512,256]{1,0:T(8,128)(2,1)}) %reduce-scatter.36.cloned.1.call-update) | async-done | bytes 262160 | tf_op jit(solution)/shard_map/reduce_scatter | solution.py:452
  1569.1 25.3 %reduce-scatter.32.cloned.1.call-done = bf16[512,64]{0,1:T(8,128)(2,1)} async-done(((bf16[2048,64]{0,1:T(8,128)(2,1)}), bf16[512,64]{0,1:T(8,128)(2,1)}) %reduce-scatter.32.cloned.1.call-update) | async-done | bytes 65552 | tf_op jit(solution)/shard_map/reduce_scatter | solution.py:440
  1596.0 25.6 %reduce-scatter.34.cloned.1.call-done = bf16[512,64]{0,1:T(8,128)(2,1)} async-done(((bf16[2048,64]{0,1:T(8,128)(2,1)}), bf16[512,64]{0,1:T(8,128)(2,1)}) %reduce-scatter.34.cloned.1.call-update) | async-done | bytes 65552 | tf_op jit(solution)/shard_map/reduce_scatter | solution.py:446
  1623.1 29.9 %reduce-scatter.30.cloned.1.call-done = bf16[512,256]{0,1:T(8,128)(2,1)} async-done(((bf16[2048,256]{0,1:T(8,128)(2,1)}), bf16[512,256]{0,1:T(8,128)(2,1)}) %reduce-scatter.30.cloned.1.call-update) | async-done | bytes 262160 | tf_op jit(solution)/shard_map/reduce_scatter | solution.py:434
  1654.9 89.8 %reduce-scatter.28.cloned.1.call-done = bf16[256,2048]{1,0:T(8,128)(2,1)} async-done(((bf16[2048,2048]{1,0:T(8,128)(2,1)}), bf16[256,2048]{1,0:T(8,128)(2,1)}) %reduce-scatter.28.cloned.1.call-update) | async-done | bytes 1048592 | tf_op jit(solution)/shard_map/reduce_scatter | solution.py:109
  1748.5 38.8 %all-reduce.20 = (f32[2048]{0:T(1024)S(1)}, f32[256]{0:T(256)S(1)}, f32[256]{0:T(256)S(1)}, f32[2048]{0:T(1024)S(1)}, f32[2048]{0:T(1024)S(1)}, /*index=5*/f32[2...) all-reduce(f32[2048]{0:T(1024)S(1)} %get-tuple-element.648, ...), channel_id=19, replica_groups=mesh['row'=4,'col'=8] {'row','col'}, use_global_device_ids=true, to_apply=%region_50.51.clone | all-reduce | flops 12800 | bytes 102400
  1795.3 89.5 %reduce-scatter.48.cloned.1.call-done = f32[64,256]{1,0:T(8,128)} async-done(((f32[2048,256]{1,0:T(8,128)}), f32[64,256]{1,0:T(8,128)}) %reduce-scatter.48.cloned.1.call-update) | async-done | bytes 65552 | tf_op jit(solution)/shard_map/reduce_scatter | solution.py:474
  1884.8 137.6 %reduce-scatter.50.cloned.1.call-done = f32[64,256]{1,0:T(8,128)} async-done(((f32[2048,256]{1,0:T(8,128)}), f32[64,256]{1,0:T(8,128)}) %reduce-scatter.50.cloned.1.call-update) | async-done | bytes 65552 | tf_op jit(solution)/shard_map/reduce_scatter | solution.py:475
  2022.4 135.9 %reduce-scatter.44.cloned.1.call-done = f32[64,64]{1,0:T(8,128)} async-done(((f32[2048,64]{1,0:T(8,128)}), f32[64,64]{1,0:T(8,128)}) %reduce-scatter.44.cloned.1.call-update) | async-done | bytes 16400 | tf_op jit(solution)/shard_map/reduce_scatter | solution.py:472
  2158.4 135.7 %reduce-scatter.46.cloned.1.call-done = f32[64,64]{1,0:T(8,128)} async-done(((f32[2048,64]{1,0:T(8,128)}), f32[64,64]{1,0:T(8,128)}) %reduce-scatter.46.cloned.1.call-update) | async-done | bytes 16400 | tf_op jit(solution)/shard_map/reduce_scatter | solution.py:473
  (576 shorter events, 336.2 us)
Async XLA Ops:
  8.0 72.0 %all-gather.16.cloned.1.call-start = ((), (), s32[]{:S(2)}) async-start(), calls=%async_computation.22 | async-start | bytes 1310720 | tf_op jit(solution)/shard_map/all_gather | solution.py:197
  8.8 134.5 %all-gather.14.cloned.1.call-start = ((), (), s32[]{:S(2)}) async-start(), calls=%async_computation.21 | async-start | bytes 9437184 | tf_op jit(solution)/shard_map/all_gather | solution.py:105
  58.2 273.8 %copy-start.86 = (bf16[2048]{0:T(1024)(128)(2,1)}, bf16[2048]{0:T(1024)(128)(2,1)S(1)}, u32[]{:S(2)}) copy-start(bf16[2048]{0:T(1024)(128)(2,1)S(1)} %get-tuple-element.760) | copy-start | bytes 12292
  58.2 273.8 %copy-start.84 = (bf16[2048]{0:T(1024)(128)(2,1)}, bf16[2048]{0:T(1024)(128)(2,1)S(1)}, u32[]{:S(2)}) copy-start(bf16[2048]{0:T(1024)(128)(2,1)S(1)} %get-tuple-element.759) | copy-start | bytes 12292
  58.3 373.2 %copy-start.53 = (f32[2048]{0:T(1024)}, f32[2048]{0:T(1024)S(1)}, u32[]{:S(2)}) copy-start(f32[2048]{0:T(1024)S(1)} %convert_element_type.213) | copy-start | bytes 24580
  59.9 371.7 %copy-start.76 = (f32[256]{0:T(256)}, f32[256]{0:T(256)S(1)}, u32[]{:S(2)}) copy-start(f32[256]{0:T(256)S(1)} %fusion.126) | copy-start | bytes 3076
  61.2 143.5 %all-gather.20.cloned.1.call-start = ((), (), s32[]{:S(2)}) async-start(), calls=%async_computation.24 | async-start | bytes 2359296 | tf_op jit(solution)/shard_map/all_gather | solution.py:228
  152.4 46.9 %all-to-all-start = ((bf16[8,256,256]{1,2,0:T(8,128)(2,1)}), bf16[8,256,256]{1,2,0:T(8,128)(2,1)S(1)}, u32[]{:S(2)}, u32[]{:S(2)}) async-start(bf16[8,256,256]{1,2,0:T(8,128)(2,1)} %bitcast.244), calls=%async_computation | async-start | bytes 2097152 | tf_op jit(solution)/shard_map/all_to_all | solution.py:138
  156.0 89.0 %all-gather.18.cloned.1.call-start = ((), (), s32[]{:S(2)}) async-start(), calls=%async_computation.23 | async-start | bytes 2359296 | tf_op jit(solution)/shard_map/all_gather | solution.py:229
  289.3 33.8 %all-to-all-start.1 = ((bf16[256,8,256]{2,0,1:T(8,128)(2,1)}), bf16[256,8,256]{2,0,1:T(8,128)(2,1)S(1)}, u32[]{:S(2)}, u32[]{:S(2)}) async-start(bf16[256,8,256]{2,0,1:T(8,128)(2,1)} %bitcast.327), calls=%async_computation.1 | async-start | bytes 2097152 | tf_op jit(solution)/shard_map/all_to_all | solution.py:142
  292.8 30.3 %all-gather.22.cloned.1.call-start = ((), (), s32[]{:S(2)}) async-start(), calls=%async_computation.25 | async-start | bytes 1310720 | tf_op jit(solution)/shard_map/all_gather | solution.py:200
  293.4 136.5 %reduce-scatter.20.cloned.1.call-start = ((), (), s32[]{:S(2)}) async-start(), calls=%async_computation.26 | async-start | bytes 9437184 | tf_op jit(solution)/shard_map/reduce_scatter | solution.py:122
  330.5 94.3 %copy-start.7 = (bf16[256,2048]{1,0:T(8,128)(2,1)S(1)}, bf16[256,2048]{1,0:T(8,128)(2,1)}, u32[]{:S(2)}) copy-start(bf16[256,2048]{1,0:T(8,128)(2,1)} %param.31) | copy-start | bytes 3145732
  330.5 152.2 %all-gather.26.cloned.1.call-start = ((), (), s32[]{:S(2)}) async-start(), calls=%async_computation.28 | async-start | bytes 5242880 | tf_op jit(solution)/shard_map/all_gather | solution.py:201
  331.2 205.9 %all-gather.28.cloned.1.call-start = ((), (), s32[]{:S(2)}) async-start(), calls=%async_computation.29 | async-start | bytes 5242880 | tf_op jit(solution)/shard_map/all_gather | solution.py:202
  332.0 289.4 %all-gather.24.cloned.1.call-start = ((), (), s32[]{:S(2)}) async-start(), calls=%async_computation.27 | async-start | bytes 9437184 | tf_op jit(solution)/shard_map/all_gather | solution.py:105
  436.4 237.8 %all-gather.30.cloned.1.call-start = ((), (), s32[]{:S(2)}) async-start(), calls=%async_computation.30 | async-start | bytes 5242880 | tf_op jit(solution)/shard_map/all_gather | solution.py:203
  436.9 343.1 %reduce-scatter.22.cloned.1.call-start = ((), (), s32[]{:S(2)}) async-start(), calls=%async_computation.31 | async-start | bytes 9437184 | tf_op jit(solution)/shard_map/reduce_scatter | solution.py:122
  688.2 104.7 %all-gather.32.cloned.1.call-start = ((), (), s32[]{:S(2)}) async-start(), calls=%async_computation.32 | async-start | bytes 1081344 | tf_op jit(solution)/shard_map/all_gather | solution.py:178
  688.8 159.7 %all-gather.34.cloned.1.call-start = ((), (), s32[]{:S(2)}) async-start(), calls=%async_computation.33 | async-start | bytes 1081344 | tf_op jit(solution)/shard_map/all_gather | solution.py:179
  689.4 252.0 %all-gather.36.cloned.1.call-start = ((), (), s32[]{:S(2)}) async-start(), calls=%async_computation.34 | async-start | bytes 9437184 | tf_op jit(solution)/shard_map/all_gather | solution.py:131
  860.2 217.8 %reduce-scatter.24.cloned.1.call-start = ((), (), s32[]{:S(2)}) async-start(), calls=%async_computation.35 | async-start | bytes 9437184 | tf_op jit(solution)/shard_map/reduce_scatter | solution.py:109
  989.9 90.9 %copy-start.14 = (bf16[256,2048]{1,0:T(8,128)(2,1)S(1)}, bf16[256,2048]{1,0:T(8,128)(2,1)}, u32[]{:S(2)}) copy-start(bf16[256,2048]{1,0:T(8,128)(2,1)} %reduce-scatter.20.cloned.1.call-done) | copy-start | bytes 3145732
  989.9 90.9 %copy-start.89 = (f32[256]{0:T(256)S(1)}, f32[256]{0:T(256)}, u32[]{:S(2)}) copy-start(f32[256]{0:T(256)} %copy-done.88) | copy-start | bytes 3076
  989.9 178.5 %all-gather.38.cloned.1.call-start = ((), (), s32[]{:S(2)}) async-start(), calls=%async_computation.36 | async-start | bytes 9437184 | tf_op jit(solution)/shard_map/all_gather | solution.py:131
  1175.1 31.0 %all-to-all-start.2 = ((bf16[8,256,256]{2,1,0:T(8,128)(2,1)}), bf16[8,256,256]{2,1,0:T(8,128)(2,1)}, u32[]{:S(2)}, u32[]{:S(2)}) async-start(bf16[8,256,256]{2,1,0:T(8,128)(2,1)} %bitcast.13), calls=%async_computation.5 | async-start | bytes 2097152 | tf_op jit(solution)/shard_map/all_to_all | solution.py:138
  1179.5 215.7 %reduce-scatter.52.cloned.1.call-start = ((), (), s32[]{:S(2)}) async-start(), calls=%async_computation.50 | async-start | bytes 2359296
  1299.2 97.3 %reduce-scatter.26.cloned.1.call-start = ((), (), s32[]{:S(2)}) async-start(), calls=%async_computation.37 | async-start | bytes 2359296 | tf_op jit(solution)/shard_map/reduce_scatter | solution.py:421
  1318.2 109.4 %reduce-scatter.42.cloned.1.call-start = ((), (), s32[]{:S(2)}) async-start(), calls=%async_computation.45 | async-start | bytes 5242880 | tf_op jit(solution)/shard_map/reduce_scatter | solution.py:467
  1332.4 148.7 %reduce-scatter.38.cloned.1.call-start = ((), (), s32[]{:S(2)}) async-start(), calls=%async_computation.43 | async-start | bytes 5242880 | tf_op jit(solution)/shard_map/reduce_scatter | solution.py:455
  1359.9 176.8 %reduce-scatter.40.cloned.1.call-start = ((), (), s32[]{:S(2)}) async-start(), calls=%async_computation.44 | async-start | bytes 5242880 | tf_op jit(solution)/shard_map/reduce_scatter | solution.py:461
  1364.3 30.2 %all-to-all-start.3 = ((bf16[256,8,256]{0,2,1:T(8,128)(2,1)}), bf16[256,8,256]{0,2,1:T(8,128)(2,1)S(1)}, u32[]{:S(2)}, u32[]{:S(2)}) async-start(bf16[256,8,256]{0,2,1:T(8,128)(2,1)} %fusion.96), calls=%async_computation.6 | async-start | bytes 2097152 | tf_op jit(solution)/shard_map/all_to_all | solution.py:142
  1368.0 199.3 %reduce-scatter.36.cloned.1.call-start = ((), (), s32[]{:S(2)}) async-start(), calls=%async_computation.42 | async-start | bytes 1310720 | tf_op jit(solution)/shard_map/reduce_scatter | solution.py:452
  1375.1 219.4 %reduce-scatter.32.cloned.1.call-start = ((), (), s32[]{:S(2)}) async-start(), calls=%async_computation.40 | async-start | bytes 327680 | tf_op jit(solution)/shard_map/reduce_scatter | solution.py:440
  1406.6 215.0 %reduce-scatter.34.cloned.1.call-start = ((), (), s32[]{:S(2)}) async-start(), calls=%async_computation.41 | async-start | bytes 327680 | tf_op jit(solution)/shard_map/reduce_scatter | solution.py:446
  1407.3 245.7 %reduce-scatter.30.cloned.1.call-start = ((), (), s32[]{:S(2)}) async-start(), calls=%async_computation.39 | async-start | bytes 1310720 | tf_op jit(solution)/shard_map/reduce_scatter | solution.py:434
  1408.4 336.3 %reduce-scatter.28.cloned.1.call-start = ((), (), s32[]{:S(2)}) async-start(), calls=%async_computation.38 | async-start | bytes 9437184 | tf_op jit(solution)/shard_map/reduce_scatter | solution.py:109
  1418.2 466.7 %reduce-scatter.48.cloned.1.call-start = ((), (), s32[]{:S(2)}) async-start(), calls=%async_computation.48 | async-start | bytes 2162688 | tf_op jit(solution)/shard_map/reduce_scatter | solution.py:474
  1421.2 601.2 %reduce-scatter.50.cloned.1.call-start = ((), (), s32[]{:S(2)}) async-start(), calls=%async_computation.49 | async-start | bytes 2162688 | tf_op jit(solution)/shard_map/reduce_scatter | solution.py:475
  1424.5 733.8 %reduce-scatter.44.cloned.1.call-start = ((), (), s32[]{:S(2)}) async-start(), calls=%async_computation.46 | async-start | bytes 1081344 | tf_op jit(solution)/shard_map/reduce_scatter | solution.py:472
  1427.4 866.7 %reduce-scatter.46.cloned.1.call-start = ((), (), s32[]{:S(2)}) async-start(), calls=%async_computation.47 | async-start | bytes 1081344 | tf_op jit(solution)/shard_map/reduce_scatter | solution.py:473
  1539.5 205.2 %copy-start.10 = (f32[256,2048]{1,0:T(8,128)S(1)}, f32[256,2048]{1,0:T(8,128)}, u32[]{:S(2)}) copy-start(f32[256,2048]{1,0:T(8,128)} %copy-done.9) | copy-start | bytes 6291460
  1654.9 93.5 %copy-start.78 = (f32[2048]{0:T(1024)S(1)}, f32[2048]{0:T(1024)}, u32[]{:S(2)}) copy-start(f32[2048]{0:T(1024)} %get-tuple-element.638) | copy-start | bytes 24580
  1654.9 93.5 %copy-start.79 = (f32[2048]{0:T(1024)S(1)}, f32[2048]{0:T(1024)}, u32[]{:S(2)}) copy-start(f32[2048]{0:T(1024)} %get-tuple-element.642) | copy-start | bytes 24580
  1654.9 93.5 %copy-start.80 = (f32[2048]{0:T(1024)S(1)}, f32[2048]{0:T(1024)}, u32[]{:S(2)}) copy-start(f32[2048]{0:T(1024)} %get-tuple-element.636) | copy-start | bytes 24580
  1654.9 93.5 %copy-start.81 = (f32[2048]{0:T(1024)S(1)}, f32[2048]{0:T(1024)}, u32[]{:S(2)}) copy-start(f32[2048]{0:T(1024)} %get-tuple-element.651) | copy-start | bytes 24580
  1654.9 93.6 %copy-start.110 = (f32[2048]{0:T(1024)S(1)}, f32[2048]{0:T(1024)}, u32[]{:S(2)}) copy-start(f32[2048]{0:T(1024)} %get-tuple-element.640) | copy-start | bytes 24580
  1654.9 137.0 %copy-start.101 = (f32[256]{0:T(256)S(1)}, f32[256]{0:T(256)}, u32[]{:S(2)}) copy-start(f32[256]{0:T(256)} %copy-done.100) | copy-start | bytes 3076
  (104 other events, 1719.9 us)
Sparse Core Ops, SparseCore 0:
  10.7 29.6 all-gather.15
  61.3 81.9 all-gather.13
  151.4 47.5 all-gather.19
  201.1 27.2 all-gather.17
  295.2 27.8 all-gather.21
  330.6 99.3 reduce-scatter.19
  431.8 50.8 all-gather.25
  484.5 52.5 all-gather.27
  539.3 82.0 all-gather.23
  623.0 51.0 all-gather.29
  688.3 91.6 reduce-scatter.21
  860.4 80.9 all-gather.35
  990.0 88.0 reduce-scatter.23
  1087.9 80.4 all-gather.37
  1299.3 34.8 reduce-scatter.51
  1336.9 34.7 reduce-scatter.25
  1374.5 50.9 reduce-scatter.41
  1428.4 52.5 reduce-scatter.37
  1484.0 52.5 reduce-scatter.39
  1539.4 27.9 reduce-scatter.35
  1570.1 24.3 reduce-scatter.31
  1597.2 24.3 reduce-scatter.33
  1625.1 27.9 reduce-scatter.29
  1655.2 89.5 reduce-scatter.27
  1747.6 137.2 reduce-scatter.47
  1887.5 134.8 reduce-scatter.49
  2025.1 133.2 reduce-scatter.43
  2161.2 132.8 reduce-scatter.45
Sparse Core Ops, SparseCore 1:
  691.7 101.1 all-gather.31
  795.8 52.7 all-gather.33
where the time goes:
time: 2310 us; the launch traced here: 2300 us
  waiting for transfers between devices  1580 us (68%)
  matrix products  287 us (12%)
  blocking collectives  192 us (8%)
  other arithmetic  107 us (5%)
  local copies, waits for them, and re-layouts  88.2 us (4%)
    reduce_scatter x2, waiting for transfers between devices, column_input_grad(): lax.psum_scatter(product_t(grad_rows, weight_cols).astype(jnp.bfloat16),...  177 us
    all_gather x2, waiting for transfers between devices, row_grads(): shard_piece = lax.all_gather(grad_own, 'col', axis=0, tiled=True)  162 us
    all_gather x2, waiting for transfers between devices, column_inputs(): lax.all_gather(own_rows, 'col', axis=0, tiled=True)  143 us
    reduce_scatter x1, waiting for transfers between devices, local(): lax.psum_scatter(layer_proj_grad, ('row', 'col'), scatter_dimension=0, ti...  138 us
    reduce_scatter x1, waiting for transfers between devices, local(): lax.psum_scatter(laurel_down_grad, ('row', 'col'), scatter_dimension=0, t...  136 us
    reduce_scatter x1, waiting for transfers between devices, local(): lax.psum_scatter(laurel_up_grad, ('row', 'col'), scatter_dimension=0, til...  136 us
    reduce_scatter x2, waiting for transfers between devices, row_output(): lax.psum_scatter(product_t(hidden_rows, weight_cols).astype(jnp.bfloat16)...  92.6 us
    reduce_scatter x1, waiting for transfers between devices, local(): lax.psum_scatter(layer_gate_grad, ('row', 'col'), scatter_dimension=0, ti...  89.5 us
  transfers between devices with their start and end apart: 34, of which 27 were waited for; matrix products, arithmetic and copies ran while one was open for 11% of the time, Pallas kernels for 0%

commit v1 on v0

v1 whole, which is shorter than its diff:
```python
from functools import partial
import math

import jax
import jax.numpy as jnp
from jax import lax
from jax.experimental import pallas as pl
from jax.experimental.pallas import tpu as pltpu
from jax.sharding import PartitionSpec as P

HEADS = 8
KV_HEADS = 2
HEAD = 256
BLOCK = 256


NORM_EPS = 1e-06
ROOT_HALF = 0.7071067811865476
ROPE_THETA = 1000000.0


def rms_scale(values, scale_gain):
    return (
        values
        * lax.rsqrt(jnp.mean(values * values, axis=-1, keepdims=True) + NORM_EPS)
        * scale_gain
    )


def rms_plain(values):
    return values * lax.rsqrt(jnp.mean(values * values, axis=-1, keepdims=True) + NORM_EPS)


def rotate(values, position):
    half_width = values.shape[-1] // 2
    steps_up = jnp.arange(half_width, dtype=jnp.float32)
    frequency = jnp.exp(steps_up * (-2.0 * math.log(ROPE_THETA) / values.shape[-1]))
    angle_grid = position.astype(jnp.float32)[:, None] * frequency[None, :]
    cosine = jnp.cos(angle_grid)[:, None, :]
    sine_part = jnp.sin(angle_grid)[:, None, :]
    first_half = values[..., :half_width]
    second_half = values[..., half_width:]
    return jnp.concatenate(
        [
            first_half * cosine - second_half * sine_part,
            second_half * cosine + first_half * sine_part,
        ],
        axis=-1,
    )


def head_prepare(projected, head_gain, position):
    shaped = projected.reshape(projected.shape[0], -1, HEAD)
    return rotate(rms_scale(shaped, head_gain), position)


def placement_info(lengths, tokens_at):
    finish = jnp.cumsum(lengths)
    begins = finish - lengths
    segment = jnp.sum((tokens_at[:, None] >= finish[None, :]).astype(jnp.int32), axis=1)
    chosen = segment[:, None] == jnp.arange(lengths.shape[0], dtype=jnp.int32)[None, :]
    begin = jnp.sum(jnp.where(chosen, begins[None, :], 0), axis=1)
    end = jnp.sum(jnp.where(chosen, finish[None, :], 0), axis=1)
    position = tokens_at - begin
    reach = jnp.minimum(end, begin + (position // BLOCK + 1) * BLOCK)
    return (position, begin, reach)


def geglu(gate_in, up_in):
    return jax.nn.gelu(gate_in, approximate=True) * up_in


def residual_mix(inputs, attention_out, normed, laurel_out, attention_gain, laurel_gain, pre_gain):
    mixed = (
        inputs
        + rms_scale(attention_out, attention_gain)
        + normed
        + rms_scale(laurel_out, laurel_gain)
    ) * ROOT_HALF
    return (mixed, rms_scale(mixed, pre_gain))


def feed_mix(mixed, down_out, post_gain):
    return mixed + rms_scale(down_out, post_gain)


def final_mix(after_feed, per_out, final_gain):
    return after_feed + rms_scale(per_out, final_gain)


def product(left, right):
    return jnp.dot(left, right, preferred_element_type=jnp.float32)


def product_t(left, right):
    return lax.dot_general(
        left, right, (((1,), (1,)), ((), ())), preferred_element_type=jnp.float32
    )


def product_tn(left, right):
    return lax.dot_general(
        left, right, (((0,), (0,)), ((), ())), preferred_element_type=jnp.float32
    )


def hop(values, axis, mask):
    size = lax.axis_size(axis)
    return lax.ppermute(values, axis, [(i, i ^ mask) for i in range(size)])


def after(values, *others):
    return lax.optimization_barrier((values,) + others)[0]


def xor_blocks(values, me, count):
    width = values.shape[-1] // count
    blocks = [values[..., i * width : (i + 1) * width] for i in range(count)]
    bit = 1
    while bit < count:
        flip = (me & bit) != 0
        blocks = [jnp.where(flip, blocks[i ^ bit], blocks[i]) for i in range(count)]
        bit *= 2
    return jnp.concatenate(blocks, axis=-1)


def xor_gather(piece, axis, count, unit):
    if count == 4:
        half = piece.shape[0] // 2
        near = hop(piece, axis, unit)
        far = hop(piece, axis, 2 * unit)
        upper = hop(near[:half], axis, 2 * unit)
        lower = hop(far[half:], axis, unit)
        return [piece, near, far, jnp.concatenate([upper, lower], axis=0)]
    pieces = [piece]
    bit = 1
    while bit < count:
        pieces = pieces + [hop(one, axis, bit * unit) for one in pieces]
        bit *= 2
    return pieces


def add_low(left, right):
    return (left.astype(jnp.float32) + right.astype(jnp.float32)).astype(jnp.bfloat16)


def xor_scatter(parts, axis, unit):
    count = len(parts)
    if count == 4:
        half = parts[0].shape[0] // 2
        upper = hop(parts[3][:half], axis, 2 * unit)
        lower = hop(parts[3][half:], axis, unit)
        near_low = hop(parts[1][half:], axis, unit)
        far_up = hop(parts[2][:half], axis, 2 * unit)
        near_up = hop(add_low(parts[1][:half], upper), axis, unit)
        far_low = hop(add_low(parts[2][half:], lower), axis, 2 * unit)
        own = parts[0].astype(jnp.float32)
        top = own[:half] + near_up.astype(jnp.float32) + far_up.astype(jnp.float32)
        bottom = own[half:] + near_low.astype(jnp.float32) + far_low.astype(jnp.float32)
        return jnp.concatenate([top, bottom], axis=0)
    bit = count // 2
    while bit > 0:
        parts = [add_low(parts[j], hop(parts[j + bit], axis, bit * unit)) for j in range(bit)]
        bit //= 2
    return parts[0].astype(jnp.float32)


def gather_cols(shard, pairs, row_total, dep=None):
    along = xor_gather(shard, "col", pairs, 2)
    height = shard.shape[0]
    stacked = jnp.concatenate(along, axis=0)
    if dep is not None:
        stacked = after(stacked, dep)
    mine = xor_gather(stacked, "row", row_total, 1)
    other = [hop(one, "col", 1) for one in mine]
    rows = []
    for r in range(row_total):
        blocks = []
        for z in range(pairs):
            for side in (mine, other):
                blocks.append(side[r][z * height : (z + 1) * height])
        rows.append(jnp.concatenate(blocks, axis=1))
    return jnp.concatenate(rows, axis=0), mine[-1]


def gather_rows(shard, row_total, dep):
    pieces = xor_gather(after(shard, dep), "row", row_total, 1)
    return jnp.concatenate(pieces, axis=0), pieces[-1]


def scatter_rows(total, row_total):
    height = total.shape[0] // row_total
    return xor_scatter([total[r * height : (r + 1) * height] for r in range(row_total)], "row", 1)


def scatter_cols(total, row_total, pairs):
    mine = scatter_rows(total, row_total).astype(jnp.bfloat16)
    width = mine.shape[1] // pairs
    return xor_scatter([mine[:, z * width : (z + 1) * width] for z in range(pairs)], "col", 2)


def pair_columns(columns, count):
    width = columns.shape[1] // count
    keep = [columns[:, j * width : (j + 1) * width] for j in range(0, count, 2)]
    give = [columns[:, j * width : (j + 1) * width] for j in range(1, count, 2)]
    other = hop(jnp.concatenate(give, axis=1), "col", 1)
    return jnp.concatenate([jnp.concatenate(keep, axis=1), other], axis=0)


def pair_rows(own):
    return jnp.concatenate([own, hop(own, "col", 1)], axis=0)


def attend_body(span_ref, window_ref, query_ref, key_ref, value_ref, out_ref, inverse_ref, sums, weights):
    rows = query_ref.shape[0]
    low_edge = window_ref[:, 0:1]
    high_edge = window_ref[:, 1:2]
    query = query_ref[...]
    sums[...] = jnp.zeros_like(sums)
    weights[...] = jnp.zeros_like(weights)

    def one_tile(tile, carry):
        scores = lax.dot_general(
            query, key_ref[tile], (((1,), (1,)), ((), ())), preferred_element_type=jnp.float32
        )
        place = tile * rows + lax.broadcasted_iota(jnp.int32, scores.shape, 1)
        exps = jnp.where((place >= low_edge) & (place < high_edge), jnp.exp(scores), 0.0)
        part = exps[:, :128]
        for start in range(128, rows, 128):
            part = part + exps[:, start : start + 128]
        weights[...] += part
        sums[...] += jnp.dot(
            exps.astype(jnp.bfloat16), value_ref[tile], preferred_element_type=jnp.float32
        )
        return carry

    lax.fori_loop(span_ref[0], span_ref[1], one_tile, 0)
    inverse = 1.0 / jnp.sum(weights[...], axis=1, keepdims=True)
    out_ref[...] = (sums[...] * inverse).astype(jnp.bfloat16)
    inverse_ref[...] = jnp.broadcast_to(inverse, inverse_ref.shape)


def attend(span, window, query, gathered):
    rows, width = query.shape
    tiles = gathered.shape[0]
    groups = HEADS // KV_HEADS
    half = pl.BlockSpec((rows, HEAD), lambda h, s: (0, h))
    flops = 4 * rows * rows * tiles * width
    return pl.pallas_call(
        attend_body,
        out_shape=(
            jax.ShapeDtypeStruct((rows, width), jnp.bfloat16),
            jax.ShapeDtypeStruct((rows, HEADS * 128), jnp.float32),
        ),
        grid_spec=pltpu.PrefetchScalarGridSpec(
            num_scalar_prefetch=1,
            grid=(HEADS,),
            in_specs=[
                pl.BlockSpec((rows, 2), lambda h, s: (0, 0)),
                half,
                pl.BlockSpec((tiles, None, rows, HEAD), lambda h, s: (0, 0, 0, h // groups)),
                pl.BlockSpec((tiles, None, rows, HEAD), lambda h, s: (0, 1, 0, h // groups)),
            ],
            out_specs=(half, pl.BlockSpec((rows, 128), lambda h, s: (0, h))),
            scratch_shapes=[
                pltpu.VMEM((rows, HEAD), jnp.float32),
                pltpu.VMEM((rows, 128), jnp.float32),
            ],
        ),
        cost_estimate=pl.CostEstimate(
            flops=flops, transcendentals=rows * rows * tiles * HEADS, bytes_accessed=8 * rows * width
        ),
        name="attend",
    )(span, window, query, gathered, gathered)


def attend_back_body(
    span_ref, window_ref, query_ref, key_ref, value_ref, grad_ref, out_ref, inverse_ref,
    query_grad_ref, pair_grad_ref, query_sum, key_sum, value_sum,
):
    rows = query_ref.shape[0]
    groups = HEADS // KV_HEADS
    head = pl.program_id(0)
    low_edge = window_ref[0:1, :]
    high_edge = window_ref[1:2, :]
    query = query_ref[...]
    grad_wide = grad_ref[...].astype(jnp.float32)
    inverse = inverse_ref[:, 0:1]
    delta = jnp.sum(grad_wide * out_ref[...].astype(jnp.float32), axis=1, keepdims=True) * inverse
    delta_row = jnp.transpose(jnp.broadcast_to(delta, (rows, 128)))[0:1, :]
    grad_scaled = (grad_wide * inverse).astype(jnp.bfloat16)
    query_sum[...] = jnp.zeros_like(query_sum)

    @pl.when(lax.rem(head, groups) == 0)
    def _():
        key_sum[...] = jnp.zeros_like(key_sum)
        value_sum[...] = jnp.zeros_like(value_sum)

    def one_tile(tile, carry):
        keys = key_ref[tile]
        contract_last = (((1,), (1,)), ((), ()))
        scores = lax.dot_general(keys, query, contract_last, preferred_element_type=jnp.float32)
        place = tile * rows + lax.broadcasted_iota(jnp.int32, scores.shape, 0)
        exps = jnp.where((place >= low_edge) & (place < high_edge), jnp.exp(scores), 0.0)
        prob_grad = lax.dot_general(
            value_ref[tile], grad_scaled, contract_last, preferred_element_type=jnp.float32
        )
        score_grad = (exps * (prob_grad - delta_row)).astype(jnp.bfloat16)
        key_sum[tile] += jnp.dot(score_grad, query, preferred_element_type=jnp.float32)
        value_sum[tile] += jnp.dot(
            exps.astype(jnp.bfloat16), grad_scaled, preferred_element_type=jnp.float32
        )
        query_sum[...] += lax.dot_general(
            score_grad, keys, (((0,), (0,)), ((), ())), preferred_element_type=jnp.float32
        )
        return carry

    lax.fori_loop(span_ref[0], span_ref[1], one_tile, 0)
    query_grad_ref[...] = query_sum[...] * (1.0 / math.sqrt(HEAD))

    @pl.when(lax.rem(head, groups) == groups - 1)
    def _():
        pair_grad_ref[:, 0] = key_sum[...].astype(jnp.bfloat16)
        pair_grad_ref[:, 1] = value_sum[...].astype(jnp.bfloat16)


def attend_back(span, window, query, gathered, grad, out, inverse):
    rows, width = query.shape
    tiles = gathered.shape[0]
    groups = HEADS // KV_HEADS
    half = pl.BlockSpec((rows, HEAD), lambda h, s: (0, h))
    return pl.pallas_call(
        attend_back_body,
        out_shape=(
            jax.ShapeDtypeStruct((rows, width), jnp.float32),
            jax.ShapeDtypeStruct(gathered.shape, jnp.bfloat16),
        ),
        grid_spec=pltpu.PrefetchScalarGridSpec(
            num_scalar_prefetch=1,
            grid=(HEADS,),
            in_specs=[
                pl.BlockSpec((2, rows), lambda h, s: (0, 0)),
                half,
                pl.BlockSpec((tiles, None, rows, HEAD), lambda h, s: (0, 0, 0, h // groups)),
                pl.BlockSpec((tiles, None, rows, HEAD), lambda h, s: (0, 1, 0, h // groups)),
                half,
                half,
                pl.BlockSpec((rows, 128), lambda h, s: (0, h)),
            ],
            out_specs=(
                half,
                pl.BlockSpec((tiles, 2, rows, HEAD), lambda h, s: (0, 0, 0, h // groups)),
            ),
            scratch_shapes=[
                pltpu.VMEM((rows, HEAD), jnp.float32),
                pltpu.VMEM((tiles, rows, HEAD), jnp.float32),
                pltpu.VMEM((tiles, rows, HEAD), jnp.float32),
            ],
        ),
        cost_estimate=pl.CostEstimate(
            flops=10 * rows * rows * tiles * width,
            transcendentals=rows * rows * tiles * HEADS,
            bytes_accessed=16 * rows * width,
        ),
        name="attend_back",
    )(span, window, query, gathered, gathered, grad, out, inverse)


def local(
    layer_input,
    per_layer_input,
    out_cotangent,
    seq_lengths,
    query_weight,
    key_weight,
    value_weight,
    out_weight,
    gate_weight,
    up_weight,
    down_weight,
    laurel_down,
    laurel_up,
    per_layer_gate,
    per_layer_projection,
    input_gain,
    query_gain,
    key_gain,
    attention_gain,
    laurel_gain,
    pre_feed_gain,
    post_feed_gain,
    per_layer_gain,
):
    rows, width = layer_input.shape
    row_total = lax.axis_size("row")
    col_total = lax.axis_size("col")
    pairs = col_total // 2
    me_row = lax.axis_index("row")
    me_col = lax.axis_index("col")
    rank = laurel_down.shape[1]
    embed = per_layer_gate.shape[1]
    kv_width = key_weight.shape[1]
    feed_width = gate_weight.shape[1]
    low = jnp.bfloat16
    wide = jnp.float32

    kv_all, kv_last = gather_cols(
        jnp.concatenate([key_weight, value_weight], axis=1), pairs, row_total
    )
    query_all, query_last = gather_cols(query_weight, pairs, row_total, kv_last)

    small_rows = laurel_down.shape[0]
    head_part = query_gain.shape[0]
    gains_own = jnp.concatenate(
        [
            input_gain,
            attention_gain,
            laurel_gain,
            pre_feed_gain,
            post_feed_gain,
            per_layer_gain,
            query_gain,
            key_gain,
        ]
    )
    gain_total = gains_own.shape[0]
    matrices_own = jnp.concatenate(
        [laurel_down, laurel_up, per_layer_gate, per_layer_projection], axis=1
    )
    small_width = matrices_own.shape[1]
    gains_block = jnp.pad(gains_own[None, :], ((0, 15), (0, small_width - gain_total)))
    small_own = jnp.concatenate([matrices_own, gains_block], axis=0)
    small_group = lax.all_gather(small_own, "col", axis=0, tiled=True)
    small_pieces = xor_gather(small_group, "row", row_total, 1)
    small_pieces = [one.reshape(col_total, small_rows + 16, small_width) for one in small_pieces]
    matrices = jnp.concatenate(
        [one[:, :small_rows].reshape(-1, small_width) for one in small_pieces], axis=0
    )
    laurel_down_all = matrices[:, :rank]
    laurel_up_all = matrices[:, rank : 2 * rank]
    layer_gate_all = matrices[:, 2 * rank : 2 * rank + embed]
    layer_proj_all = matrices[:, 2 * rank + embed :]
    gain_rows = [one[:, small_rows, :].astype(wide) for one in small_pieces]
    gain_list = [
        jnp.concatenate(
            [one[:, i * small_rows : (i + 1) * small_rows].reshape(-1) for one in gain_rows]
        )
        for i in range(6)
    ]
    head_gains = []
    for i in range(2):
        start = 6 * small_rows + i * head_part
        rel = jnp.concatenate([one[:, start : start + head_part].reshape(-1) for one in gain_rows])
        head_gains.append(xor_blocks(rel, me_row, row_total))

    out_all, out_last = gather_cols(out_weight, pairs, row_total, query_last)
    feed_all, feed_last = gather_rows(
        jnp.concatenate([gate_weight, up_weight], axis=1), row_total, out_last
    )
    down_all, down_last = gather_rows(down_weight, row_total, feed_last)

    tokens_at = me_col * rows + jnp.arange(rows, dtype=jnp.int32)
    position, begin, reach = placement_info(seq_lengths[0], tokens_at)
    window = jnp.stack([begin, reach])
    span = jnp.stack([jnp.min(begin) // rows, (jnp.max(reach) + rows - 1) // rows])
    inputs = xor_blocks(layer_input, me_row, row_total).astype(wide)
    cotangent = xor_blocks(out_cotangent, me_row, row_total).astype(wide)
    normed, input_pull = jax.vjp(rms_scale, inputs, gain_list[0])
    normed_low = normed.astype(low)
    kv_own = xor_blocks(product(normed_low, kv_all).astype(low), me_col, col_total)
    kv_own = kv_own.reshape(rows, col_total, 2 * kv_width)
    key_own = kv_own[:, :, :kv_width].reshape(rows, KV_HEADS * HEAD)
    value_own = kv_own[:, :, kv_width:].reshape(rows, KV_HEADS * HEAD)
    key_rot, key_pull = jax.vjp(
        partial(head_prepare, position=position), key_own.astype(wide), head_gains[1]
    )
    value_normed, value_pull = jax.vjp(
        rms_plain, value_own.astype(wide).reshape(rows, KV_HEADS, HEAD)
    )
    pair_own = jnp.stack(
        [
            key_rot.astype(low).reshape(rows, KV_HEADS * HEAD),
            value_normed.astype(low).reshape(rows, KV_HEADS * HEAD),
        ]
    )
    pair_all = lax.all_gather(pair_own, "col", axis=0, tiled=True)
    pair_all = pair_all.reshape(col_total, 2, rows, KV_HEADS * HEAD)
    query_own = xor_blocks(product(normed_low, query_all).astype(low), me_col, col_total)
    query_rot, query_pull = jax.vjp(
        partial(head_prepare, position=position), query_own.astype(wide), head_gains[0]
    )
    query_scaled = query_rot.astype(low).reshape(rows, HEADS * HEAD) * low(1.0 / math.sqrt(HEAD))
    attended, inverse = attend(span, jnp.transpose(window), query_scaled, pair_all)
    attended_rel = xor_blocks(attended, me_col, col_total)
    attention_out = product_t(attended_rel, out_all)
    laurel_mid = product(normed_low, laurel_down_all).astype(low)
    laurel_out = product_t(laurel_mid, laurel_up_all)
    (mixed, feed_in), mix_pull = jax.vjp(
        residual_mix,
        inputs,
        attention_out,
        normed_low.astype(wide),
        laurel_out,
        gain_list[1],
        gain_list[2],
        gain_list[3],
    )
    feed_low = feed_in.astype(low)
    feed_tokens = lax.all_gather(feed_low, "col", axis=0, tiled=True)
    gate_up = product(feed_tokens, feed_all).astype(low)
    gate = gate_up[:, :feed_width].astype(wide)
    up = gate_up[:, feed_width:].astype(wide)
    hidden, hidden_pull = jax.vjp(geglu, gate, up)
    hidden_low = hidden.astype(low)
    down_out = lax.psum_scatter(
        product_t(hidden_low, down_all).astype(low), "col", scatter_dimension=0, tiled=True
    ).astype(wide)
    after_feed, feed_pull = jax.vjp(feed_mix, mixed, down_out, gain_list[4])
    after_low = after_feed.astype(low)
    per_pre = product(after_low, layer_gate_all)
    per_hidden, per_pull = jax.vjp(geglu, per_pre, per_layer_input.astype(wide))
    per_low = per_hidden.astype(low)
    per_out = product_t(per_low, layer_proj_all)
    output, final_pull = jax.vjp(final_mix, after_feed, per_out, gain_list[5])
    after_grad, per_out_grad, final_gain_grad = final_pull(cotangent)
    per_out_low = per_out_grad.astype(low)
    per_hidden_grad = product(per_out_low, layer_proj_all)
    layer_proj_grad = product_tn(per_out_low, per_low)
    per_pre_grad, embed_grad = per_pull(per_hidden_grad)
    per_pre_low = per_pre_grad.astype(low)
    after_grad = after_grad + product_t(per_pre_low, layer_gate_all)
    layer_gate_grad = product_tn(after_low, per_pre_low)
    mixed_grad, down_grad, post_gain_grad = feed_pull(after_grad)
    down_low = down_grad.astype(low)
    down_tokens = lax.all_gather(down_low, "col", axis=0, tiled=True)
    hidden_grad = product(down_tokens, down_all)
    gate_grad, up_grad = hidden_pull(hidden_grad)
    feed_grad_low = jnp.concatenate([gate_grad.astype(low), up_grad.astype(low)], axis=1)
    feed_in_grad = lax.psum_scatter(
        product_t(feed_grad_low, feed_all).astype(low), "col", scatter_dimension=0, tiled=True
    ).astype(wide)
    down_total = product_tn(down_tokens, hidden_low).astype(low)
    down_weight_grad = scatter_rows(down_total, row_total)
    feed_total = product_tn(feed_tokens, feed_grad_low).astype(low)
    feed_weight_grad = scatter_rows(feed_total, row_total)
    (
        inputs_grad,
        attention_grad,
        normed_grad,
        laurel_out_grad,
        attention_gain_grad,
        laurel_gain_grad,
        pre_gain_grad,
    ) = mix_pull((mixed_grad, feed_in_grad))
    attention_low = attention_grad.astype(low)
    attended_grad = xor_blocks(product(attention_low, out_all).astype(low), me_col, col_total)
    query_rot_grad, pair_parts = attend_back(
        span, window, query_scaled, pair_all, attended_grad, attended, inverse
    )
    pair_sum = lax.psum_scatter(
        pair_parts.reshape(2 * col_total, rows, KV_HEADS * HEAD),
        "col",
        scatter_dimension=0,
        tiled=True,
    ).astype(wide)
    out_total = product_tn(pair_rows(attention_low), pair_columns(attended_rel, col_total))
    out_weight_grad = scatter_cols(out_total.astype(low), row_total, pairs)
    normed_pair = pair_rows(normed_low)
    query_grad, query_gain_grad = query_pull(query_rot_grad.reshape(rows, HEADS, HEAD))
    query_rel = xor_blocks(query_grad.astype(low), me_col, col_total)
    query_total = product_tn(normed_pair, pair_columns(query_rel, col_total))
    query_weight_grad = scatter_cols(query_total.astype(low), row_total, pairs)

    laurel_out_low = laurel_out_grad.astype(low)
    laurel_mid_grad = product(laurel_out_low, laurel_up_all)
    laurel_up_grad = product_tn(laurel_out_low, laurel_mid)
    laurel_mid_low = laurel_mid_grad.astype(low)
    laurel_down_grad = product_tn(normed_low, laurel_mid_low)
    small_total = jnp.concatenate(
        [laurel_down_grad, laurel_up_grad, layer_gate_grad, layer_proj_grad], axis=1
    ).astype(low)
    small_total = small_total.reshape(row_total, col_total, small_rows, small_width)
    small_total = jnp.transpose(small_total, (1, 0, 2, 3)).reshape(-1, small_width)
    small_summed = lax.psum_scatter(small_total, "col", scatter_dimension=0, tiled=True)
    small_grad = scatter_rows(small_summed, row_total)

    normed_grad = (
        normed_grad
        + product_t(laurel_mid_low, laurel_down_all)
        + product_t(query_rel, query_all)
    )
    key_grad, key_gain_grad = key_pull(pair_sum[0].reshape(rows, KV_HEADS, HEAD))
    (value_grad,) = value_pull(pair_sum[1].reshape(rows, KV_HEADS, HEAD))
    kv_grad = jnp.concatenate(
        [
            key_grad.astype(low).reshape(rows, col_total, kv_width),
            value_grad.astype(low).reshape(rows, col_total, kv_width),
        ],
        axis=2,
    ).reshape(rows, col_total * 2 * kv_width)
    kv_rel = xor_blocks(kv_grad, me_col, col_total)
    kv_total = product_tn(normed_pair, pair_columns(kv_rel, col_total))
    kv_weight_grad = scatter_cols(kv_total.astype(low), row_total, pairs)
    normed_grad = normed_grad + product_t(kv_rel, kv_all)
    input_part, input_gain_grad = input_pull(normed_grad)
    input_total = xor_blocks((inputs_grad + input_part).astype(low), me_row, row_total)

    wide_gains = [
        input_gain_grad,
        attention_gain_grad,
        laurel_gain_grad,
        pre_gain_grad,
        post_gain_grad,
        final_gain_grad,
    ]
    gain_parts = [
        xor_blocks(one, me_row, row_total).reshape(row_total, col_total, small_rows)
        for one in wide_gains
    ] + [
        one.reshape(row_total, col_total, head_part) for one in (query_gain_grad, key_gain_grad)
    ]
    gain_sums = jnp.transpose(jnp.concatenate(gain_parts, axis=2), (1, 0, 2))
    gain_sums = gain_sums.reshape(col_total, row_total * gain_total)
    gain_sums = jnp.sum(lax.all_to_all(gain_sums, "col", 0, 0, tiled=True), axis=0)
    gain_sums = gain_sums.reshape(row_total, gain_total)
    gain_sums = jnp.sum(lax.all_to_all(gain_sums, "row", 0, 0, tiled=True), axis=0)
    gain_out = [gain_sums[i * small_rows : (i + 1) * small_rows] for i in range(6)]
    head_out = gain_sums[6 * small_rows :]
    return (
        xor_blocks(output.astype(low), me_row, row_total),
        input_total,
        embed_grad.astype(low),
        query_weight_grad,
        kv_weight_grad[:, :kv_width],
        kv_weight_grad[:, kv_width:],
        out_weight_grad,
        feed_weight_grad[:, :feed_width],
        feed_weight_grad[:, feed_width:],
        down_weight_grad,
        small_grad[:, :rank],
        small_grad[:, rank : 2 * rank],
        small_grad[:, 2 * rank : 2 * rank + embed],
        small_grad[:, 2 * rank + embed :],
        gain_out[0],
        head_out[:head_part],
        head_out[head_part:],
        gain_out[1],
        gain_out[2],
        gain_out[3],
        gain_out[4],
        gain_out[5],
    )


def solution(mesh):
    in_specs = (
        P(("row", "col"), None),
        P(("row", "col"), None),
        P(("row", "col"), None),
        P("row", None),
        P("row", "col"),
        P("row", "col"),
        P("row", "col"),
        P("row", "col"),
        P("row", "col"),
        P("row", "col"),
        P("row", "col"),
        P(("row", "col"), None),
        P(("row", "col"), None),
        P(("row", "col"), None),
        P(("row", "col"), None),
        P(("row", "col")),
        P(("row", "col")),
        P(("row", "col")),
        P(("row", "col")),
        P(("row", "col")),
        P(("row", "col")),
        P(("row", "col")),
        P(("row", "col")),
    )
    out_specs = (
        P(("row", "col"), None),
        P(("row", "col"), None),
        P(("row", "col"), None),
        P("row", "col"),
        P("row", "col"),
        P("row", "col"),
        P("row", "col"),
        P("row", "col"),
        P("row", "col"),
        P("row", "col"),
        P(("row", "col"), None),
        P(("row", "col"), None),
        P(("row", "col"), None),
        P(("row", "col"), None),
        P(("row", "col")),
        P(("row", "col")),
        P(("row", "col")),
        P(("row", "col")),
        P(("row", "col")),
        P(("row", "col")),
        P(("row", "col")),
        P(("row", "col")),
    )
    return jax.shard_map(local, mesh=mesh, in_specs=in_specs, out_specs=out_specs, check_vma=False)
```

time: 2310 us -> 1150 us (0.50)
  waiting for transfers between devices: 1580 us -> 499 us
  blocking collectives: 192 us -> 18.8 us
  starting transfers between devices: 17.2 us -> 133 us
  matrix products: 287 us -> 180 us
  local copies, waits for them, and re-layouts: 88.2 us -> 175 us
    reduce_scatter x16 -> x4, waiting for transfers between devices: 979 us -> 94.5 us  [the longest x1 94.4 us: local(): lax.psum_scatter(product_t(hidden_low, down_all).astype(low), 'col', scat...]
    all_gather x13 -> x3, waiting for transfers between devices: 511 us -> 80.4 us  [the longest x1 80.3 us: local(): down_tokens = lax.all_gather(down_low, 'col', axis=0, tiled=True)]
    ppermute x0 -> x107, waiting for transfers between devices: none -> 316 us  [hop(): return lax.ppermute(values, axis, [(i, i ^ mask) for i in range(size)])]
    ppermute x0 -> x107, starting transfers between devices: none -> 126 us  [hop(): return lax.ppermute(values, axis, [(i, i ^ mask) for i in range(size)])]
    dot_general x36 -> x0, matrix products: 97.1 us -> none  [the longest x12 25.5 us: score_block(): jnp.einsum('qhgd,khd->hgqk', query_low, key_slice(block_index, key_low),...]
    all_gather x4 -> x1, blocking collectives: 111 us -> 18.8 us  [local(): small_group = lax.all_gather(small_own, 'col', axis=0, tiled=True)]
    unnamed x2 -> x0, blocking collectives: 81.4 us -> none
    all_to_all x4 -> x2, waiting for transfers between devices: 84 us -> 8.21 us  [the longest x1 5.26 us: local(): lax.all_to_all(gain_sums, 'col', 0, 0, tiled=True)]
  transfers between devices with their start and end apart: 34 -> 116, of which waited for: 27 -> 57; matrix products, arithmetic and copies ran while one was open for 11% -> 25% of each run, Pallas kernels for 0% -> 1%
where the time goes in v1:
time: 1150 us; the launch traced here: 1140 us
  waiting for transfers between devices  499 us (43%)
  matrix products  180 us (16%)
  local copies, waits for them, and re-layouts  175 us (15%)
  starting transfers between devices  133 us (12%)
  other arithmetic  90.8 us (8%)
  Pallas kernels  22.9 us (2%)
  between operations  21.9 us (2%)
  blocking collectives  18.8 us (2%)
    ppermute x107, waiting for transfers between devices, hop(): return lax.ppermute(values, axis, [(i, i ^ mask) for i in range(size)])  316 us
    ppermute x107, starting transfers between devices, hop(): return lax.ppermute(values, axis, [(i, i ^ mask) for i in range(size)])  126 us
    reduce_scatter x1, waiting for transfers between devices, local(): lax.psum_scatter(product_t(hidden_low, down_all).astype(low), 'col', scat...  94.4 us
    unnamed x524, local copies, waits for them, and re-layouts  93 us
    all_gather x1, waiting for transfers between devices, local(): down_tokens = lax.all_gather(down_low, 'col', axis=0, tiled=True)  80.3 us
    dot_general x9, matrix products, product_t(): lax.dot_general(left, right, (((1,), (1,)), ((), ())), preferred_element_...  68.5 us
    dot_general x9, matrix products, product(): return jnp.dot(left, right, preferred_element_type=jnp.float32)  57.5 us
    dot_general x9, matrix products, product_tn(): lax.dot_general(left, right, (((0,), (0,)), ((), ())), preferred_element_...  54.1 us
  transfers between devices with their start and end apart: 116, of which 57 were waited for; matrix products, arithmetic and copies ran while one was open for 25% of the time, Pallas kernels for 1%

profile of v1, /device:TPU:0, one launch (start us, length us, event | category | flops | bytes accessed | tf_op | source)
XLA Modules:
  0.0 1141.4 jit_solution(3248868577270785901)
XLA Ops:
  21.7 5.4 concatenate.287
  28.0 18.8 %all_gather.12 = bf16[640,640]{1,0:T(8,128)(2,1)S(1)} all-gather(bf16[80,640]{1,0:T(8,128)(2,1)S(1)} %fusion.119), channel_id=1, replica_groups=mesh['row'=4,'col'=8] {'col'}, dimensions={0}, use_global_device_ids=true | all-gather | bytes 921600 | tf_op jit(solution)/shard_map/all_gather | solution.py:433
  63.9 12.0 %collective-permute-done.10 = bf16[256,128]{0,1:T(8,128)(2,1)S(1)} collective-permute-done((bf16[256,128]{0,1:T(8,128)(2,1)S(1)}, bf16[256,128]{0,1:T(8,128)(2,1)S(1)}, u32[]{:S(2)}, u32[]{:S(2)}) %collective-permute-start.10) | collective-permute-done | bytes 65568 | tf_op jit(solution)/shard_map/ppermute | solution.py:109
  76.5 3.6 collective-permute-done.11
  100.9 4.7 collective-permute-done.30
  118.5 8.2 collective-permute-done.1
  143.9 5.1 collective-permute-done.2
  205.6 16.7 %collective-permute-done.33 = bf16[2048,256]{1,0:T(8,128)(2,1)S(1)} collective-permute-done((bf16[2048,256]{1,0:T(8,128)(2,1)S(1)}, bf16[2048,256]{1,0:T(8,128)(2,1)S(1)}, u32[]{:S(2)}, u32[]{:S(2)}) %collective-permute-start.33) | collective-permute-done | bytes 1048608 | tf_op jit(solution)/shard_map/ppermute | solution.py:109
  262.3 9.7 attend.1
  278.7 9.0 multiply_reduce_fusion.7
  298.2 62.9 %collective-permute-done.44 = bf16[512,1024]{1,0:T(8,128)(2,1)S(1)} collective-permute-done((bf16[512,1024]{1,0:T(8,128)(2,1)S(1)}, bf16[512,1024]{1,0:T(8,128)(2,1)S(1)}, u32[]{:S(2)}, u32[]{:S(2)}) %collective-permute-start.44) | collective-permute-done | bytes 1048608 | tf_op jit(solution)/shard_map/ppermute | solution.py:109
  365.7 10.0 collective-permute-done.46
  383.4 14.8 %collective-permute-done.42 = bf16[256,2048]{1,0:T(8,128)(2,1)S(1)} collective-permute-done((bf16[256,2048]{1,0:T(8,128)(2,1)S(1)}, bf16[256,2048]{1,0:T(8,128)(2,1)S(1)}, u32[]{:S(2)}, u32[]{:S(2)}) %collective-permute-start.42) | collective-permute-done | bytes 1048608 | tf_op jit(solution)/shard_map/ppermute | solution.py:109
  402.4 24.0 %convolution_convert_fusion.3 = bf16[2048,2048]{0,1:T(8,128)(2,1)} fusion(bf16[2048,2048]{1,0:T(8,128)(2,1)} %all-gather.6.cloned.1.call-done, bf16[2048,2048]{1,0:T(8,128)(2,1)} %constant_dynamic-update-slice_fusion.147), kind=kOutput, calls=%fused_computation.24 | convolution fusion | flops 17184063488 | bytes 25165824 | tf_op jit(solution)/shard_map/dot_general | solution.py:92
  426.4 16.0 %convolution_convert_fusion.2 = bf16[2048,2048]{1,0:T(8,128)(2,1)} fusion(bf16[2048,1024]{1,0:T(8,128)(2,1)S(1)} %copy-done.78, bf16[2048,2048]{0,1:T(8,128)(2,1)} %convolution_convert_fusion.3), kind=kOutput, calls=%fused_computation.23 | convolution fusion | flops 8619294720 | bytes 20971520 | tf_op jit(solution)/shard_map/dot_general | solution.py:96
  448.7 94.4 %reduce-scatter.5.cloned.1.call-done = bf16[256,2048]{1,0:T(8,128)(2,1)} async-done(((bf16[2048,2048]{1,0:T(8,128)(2,1)}), bf16[256,2048]{1,0:T(8,128)(2,1)}) %reduce-scatter.5.cloned.1.call-update) | async-done | bytes 1048592 | tf_op jit(solution)/shard_map/reduce_scatter | solution.py:515
  558.1 80.3 %all-gather.8.cloned.1.call-done = bf16[2048,2048]{1,0:T(8,128)(2,1)} async-done(((bf16[256,2048]{1,0:T(8,128)(2,1)}), bf16[2048,2048]{1,0:T(8,128)(2,1)}) %all-gather.8.cloned.1.call-update) | async-done | bytes 8388624 | tf_op jit(solution)/shard_map/all_gather | solution.py:535
  638.5 23.1 %fusion.4 = (bf16[2048,1024]{0,1:T(8,128)(2,1)}, bf16[2048,1024]{0,1:T(8,128)(2,1)}) fusion(bf16[2048,2048]{0,1:T(8,128)(2,1)} %convolution_convert_fusion.3, bf16[2048,2048]{1,0:T(8,128)(2,1)} %all-gather.8.cloned.1.call-done, bf16[2048,1024]{1,0:T(8,128)(2,1)} %copy-done.77), kind=kOutput, calls=%fused_computation.11 | convolution fusion | flops 8644460544 | bytes 29360128 | tf_op jit(solution)/shard_map/dot_general | solution.py:92
  661.5 24.2 %convolution_convert_fusion.1 = bf16[2048,2048]{1,0:T(8,128)(2,1)} fusion(bf16[2048,2048]{1,0:T(8,128)(2,1)} %constant_dynamic-update-slice_fusion.147, bf16[2048,1024]{0,1:T(8,128)(2,1)} %get-tuple-element.298, bf16[2048,1024]{0,1:T(8,128)(2,1)} %get-tuple-element.297), kind=kOutput, calls=%fused_computation.22 | convolution fusion | flops 17200840704 | bytes 25165824 | tf_op jit(solution)/shard_map/dot_general | solution.py:96
  700.3 23.3 %convolution_convert_fusion = bf16[2048,2048]{1,0:T(8,128)(2,1)S(1)} fusion(bf16[2048,2048]{1,0:T(8,128)(2,1)} %all-gather.6.cloned.1.call-done, bf16[2048,1024]{0,1:T(8,128)(2,1)} %get-tuple-element.298, bf16[2048,1024]{0,1:T(8,128)(2,1)} %get-tuple-element.297), kind=kOutput, calls=%fused_computation.21 | convolution fusion | flops 17200840704 | bytes 25165824 | tf_op jit(solution)/shard_map/dot_general | solution.py:102
  728.0 14.9 %convolution_convert_fusion.6 = bf16[2048,1024]{1,0:T(8,128)(2,1)S(1)} fusion(bf16[2048,2048]{1,0:T(8,128)(2,1)} %all-gather.8.cloned.1.call-done, bf16[2048,2048]{0,1:T(8,128)(2,1)} %convolution_convert_fusion.3), kind=kOutput, calls=%fused_computation.35 | convolution fusion | flops 8617197568 | bytes 20971520 | tf_op jit(solution)/shard_map/dot_general | solution.py:102
  747.0 15.8 %collective-permute-done.95 = bf16[256,1024]{1,0:T(8,128)(2,1)S(1)} collective-permute-done((bf16[256,1024]{1,0:T(8,128)(2,1)S(1)}, bf16[256,1024]{1,0:T(8,128)(2,1)S(1)}, u32[]{:S(2)}, u32[]{:S(2)}) %collective-permute-start.95) | collective-permute-done | bytes 524320 | tf_op jit(solution)/shard_map/ppermute | solution.py:109
  768.2 30.1 %collective-permute-done.97 = bf16[256,1024]{1,0:T(8,128)(2,1)S(1)} collective-permute-done((bf16[256,1024]{1,0:T(8,128)(2,1)S(1)}, bf16[256,1024]{1,0:T(8,128)(2,1)S(1)}, u32[]{:S(2)}, u32[]{:S(2)}) %collective-permute-start.97) | collective-permute-done | bytes 524320 | tf_op jit(solution)/shard_map/ppermute | solution.py:109
  800.3 6.2 collective-permute-done.96
  808.5 4.6 collective-permute-done.100
  815.5 17.4 %collective-permute-done.94 = bf16[256,2048]{1,0:T(8,128)(2,1)S(1)} collective-permute-done((bf16[256,2048]{1,0:T(8,128)(2,1)S(1)}, bf16[256,2048]{1,0:T(8,128)(2,1)S(1)}, u32[]{:S(2)}, u32[]{:S(2)}) %collective-permute-start.94) | collective-permute-done | bytes 1048608 | tf_op jit(solution)/shard_map/ppermute | solution.py:109
  839.4 4.6 multiply_reduce_fusion
  848.0 4.1 convolution_convert_fusion.10
  854.8 13.2 %attend_back.1 = (f32[256,2048]{1,0:T(8,128)}, bf16[8,2,256,512]{3,2,1,0:T(8,128)(2,1)}) custom-call(s32[2]{0:T(128)} %pad_add_fusion.3.span_ref, s32[2,256]{1,0:T(2,128)} %get-tuple-element.520.window_ref, bf16[256,2048]{1,0:T(8,128)(2,1)} %copy.171.query_ref, bf16[8,2,256,512]{3,2,1,0:T(8,128)(2,1)} %bitcast.309, bf16[8,2,256,512]{3,2,1,0:T(8,128)(2,1)} %bitcast.310, ...), custom_call_target="tpu_custom_call" | custom-call | flops 10737418240 | bytes 8388608 | tf_op jit(solution)/shard_map/attend_back/pallas_call | solution.py:332
  882.5 6.4 copy.177
  891.8 7.8 collective-permute-start.49
  900.1 11.3 convolution_add_fusion.2
  916.4 4.1 convolution_convert_fusion.5
  924.3 9.9 collective-permute-done.50
  938.0 4.4 convolution_convert_fusion.4
  947.1 11.2 collective-permute-done.51
  958.9 12.2 %collective-permute-start.58 = (bf16[256,256]{1,0:T(8,128)(2,1)S(1)}, bf16[256,256]{1,0:T(8,128)(2,1)S(1)}, u32[]{:S(2)}, u32[]{:S(2)}) collective-permute-start(bf16[256,256]{1,0:T(8,128)(2,1)S(1)} %get-tuple-element.383), channel_id=1, source_target_pairs={{0,4},{1,5},{2,6},{3,7},{4,0},{5,1},{6,2},{7,3},{8,12},{9,13},{10,... | collective-permute-start | bytes 393224 | tf_op jit(solution)/shard_map/ppermute | solution.py:109
  971.2 7.9 collective-permute-done.77
  979.1 12.6 %collective-permute-start.56 = (bf16[256,256]{1,0:T(8,128)(2,1)S(1)}, bf16[256,256]{1,0:T(8,128)(2,1)S(1)}, u32[]{:S(2)}, u32[]{:S(2)}) collective-permute-start(bf16[256,256]{1,0:T(8,128)(2,1)S(1)} %get-tuple-element.382), channel_id=1, source_target_pairs={{0,4},{1,5},{2,6},{3,7},{4,0},{5,1},{6,2},{7,3},{8,12},{9,13},{10,... | collective-permute-start | bytes 393224 | tf_op jit(solution)/shard_map/ppermute | solution.py:109
  992.1 3.2 collective-permute-done.56
  995.4 3.4 collective-permute-done.60
  1007.7 6.4 collective-permute-done.61
  1021.8 9.3 collective-permute-done.83
  1072.0 3.4 fusion.21
  1078.2 3.3 all-to-all-start
  1082.1 5.3 all-to-all-done
  1088.0 3.2 all-to-all-start.1
  1104.3 3.9 collective-permute-done.63
  (1099 shorter events, 412.7 us)
Async XLA Ops:
  7.2 255.1 %all-gather.4.cloned.1.call-start = ((), (), s32[]{:S(2)}) async-start(), calls=%async_computation.6 | async-start | bytes 4718592 | tf_op jit(solution)/shard_map/all_gather | solution.py:486
  7.2 75.0 %collective-permute-start.4 = (bf16[512,256]{1,0:T(8,128)(2,1)}, bf16[512,256]{1,0:T(8,128)(2,1)}, u32[]{:S(2)}, u32[]{:S(2)}) collective-permute-start(bf16[512,256]{1,0:T(8,128)(2,1)} %param.27), channel_id=1, source_target_pairs={{0,2},{1,3},{2,0},{3,1},{4,6},{5,7},{6,4},{7,5},{8,10},{9,11},{10,... | collective-permute-start | bytes 786440 | tf_op jit(solution)/shard_map/ppermute | solution.py:109
  10.4 76.0 %collective-permute-start.5 = (bf16[512,256]{1,0:T(8,128)(2,1)}, bf16[512,256]{1,0:T(8,128)(2,1)}, u32[]{:S(2)}, u32[]{:S(2)}) collective-permute-start(bf16[512,256]{1,0:T(8,128)(2,1)} %param.27), channel_id=1, source_target_pairs={{0,4},{1,5},{2,6},{3,7},{4,0},{5,1},{6,2},{7,3},{8,12},{9,13},{10,... | collective-permute-start | bytes 786440 | tf_op jit(solution)/shard_map/ppermute | solution.py:109
  16.0 41.8 %collective-permute-start.8 = (bf16[512,128]{0,1:T(8,128)(2,1)}, bf16[512,128]{0,1:T(8,128)(2,1)}, u32[]{:S(2)}, u32[]{:S(2)}) collective-permute-start(bf16[512,128]{0,1:T(8,128)(2,1)} %get-tuple-element.430), channel_id=1, source_target_pairs={{0,2},{1,3},{2,0},{3,1},{4,6},{5,7},{6,4},{7,5},{8,10},{9,11},{10,... | collective-permute-start | bytes 393224 | tf_op jit(solution)/shard_map/ppermute | solution.py:109
  16.5 44.5 %collective-permute-start.9 = (bf16[512,128]{0,1:T(8,128)(2,1)}, bf16[512,128]{0,1:T(8,128)(2,1)S(1)}, u32[]{:S(2)}, u32[]{:S(2)}) collective-permute-start(bf16[512,128]{0,1:T(8,128)(2,1)} %get-tuple-element.430), channel_id=1, source_target_pairs={{0,4},{1,5},{2,6},{3,7},{4,0},{5,1},{6,2},{7,3},{8,12},{9,13},{10,... | collective-permute-start | bytes 393224 | tf_op jit(solution)/shard_map/ppermute | solution.py:109
  16.5 71.7 %collective-permute-start.28 = (bf16[512,256]{1,0:T(8,128)(2,1)}, bf16[512,256]{1,0:T(8,128)(2,1)}, u32[]{:S(2)}, u32[]{:S(2)}) collective-permute-start(bf16[512,256]{1,0:T(8,128)(2,1)} %param.30), channel_id=1, source_target_pairs={{0,2},{1,3},{2,0},{3,1},{4,6},{5,7},{6,4},{7,5},{8,10},{9,11},{10,... | collective-permute-start | bytes 786440 | tf_op jit(solution)/shard_map/ppermute | solution.py:109
  57.8 33.2 %collective-permute-start.29 = (bf16[512,256]{1,0:T(8,128)(2,1)}, bf16[512,256]{1,0:T(8,128)(2,1)S(1)}, u32[]{:S(2)}, u32[]{:S(2)}) collective-permute-start(bf16[512,256]{1,0:T(8,128)(2,1)} %param.30), channel_id=1, source_target_pairs={{0,4},{1,5},{2,6},{3,7},{4,0},{5,1},{6,2},{7,3},{8,12},{9,13},{10,... | collective-permute-start | bytes 786440 | tf_op jit(solution)/shard_map/ppermute | solution.py:109
  80.8 27.7 %collective-permute-start.12 = (bf16[2048,128]{0,1:T(8,128)(2,1)}, bf16[2048,128]{0,1:T(8,128)(2,1)}, u32[]{:S(2)}, u32[]{:S(2)}) collective-permute-start(bf16[2048,128]{0,1:T(8,128)(2,1)} %constant_dynamic-update-slice_fusion.7), channel_id=1, source_target_pairs={{0,8},{8,0},{16,24},{24,16},{1,9},{9,1},{17,25},{25,17},{2,10},{10... | collective-permute-start | bytes 1572872 | tf_op jit(solution)/shard_map/ppermute | solution.py:109
  82.3 28.9 %collective-permute-start.14 = (bf16[2048,128]{0,1:T(8,128)(2,1)}, bf16[2048,128]{0,1:T(8,128)(2,1)}, u32[]{:S(2)}, u32[]{:S(2)}) collective-permute-start(bf16[2048,128]{0,1:T(8,128)(2,1)} %constant_dynamic-update-slice_fusion.7), channel_id=1, source_target_pairs={{0,16},{8,24},{16,0},{24,8},{1,17},{9,25},{17,1},{25,9},{2,18},{10... | collective-permute-start | bytes 1572872 | tf_op jit(solution)/shard_map/ppermute | solution.py:109
  86.4 28.0 %collective-permute-start.24 = (bf16[2048,128]{0,1:T(8,128)(2,1)}, bf16[2048,128]{0,1:T(8,128)(2,1)S(1)}, u32[]{:S(2)}, u32[]{:S(2)}) collective-permute-start(bf16[2048,128]{0,1:T(8,128)(2,1)} %constant_dynamic-update-slice_fusion.7), channel_id=1, source_target_pairs={{0,1},{1,0},{2,3},{3,2},{4,5},{5,4},{6,7},{7,6},{8,9},{9,8},{10,11... | collective-permute-start | bytes 1572872 | tf_op jit(solution)/shard_map/ppermute | solution.py:109
  110.1 26.5 %collective-permute-start.13 = (bf16[1024,128]{0,1:T(8,128)(2,1)}, bf16[1024,128]{0,1:T(8,128)(2,1)S(1)}, u32[]{:S(2)}, u32[]{:S(2)}) collective-permute-start(bf16[1024,128]{0,1:T(8,128)(2,1)} %slice.2028), channel_id=1, source_target_pairs={{0,16},{8,24},{16,0},{24,8},{1,17},{9,25},{17,1},{25,9},{2,18},{10... | collective-permute-start | bytes 786440 | tf_op jit(solution)/shard_map/ppermute | solution.py:109
  114.4 44.3 %collective-permute-start.26 = (bf16[2048,128]{0,1:T(8,128)(2,1)}, bf16[2048,128]{0,1:T(8,128)(2,1)}, u32[]{:S(2)}, u32[]{:S(2)}) collective-permute-start(bf16[2048,128]{0,1:T(8,128)(2,1)} %collective-permute-done.14), channel_id=1, source_target_pairs={{0,1},{1,0},{2,3},{3,2},{4,5},{5,4},{6,7},{7,6},{8,9},{9,8},{10,11... | collective-permute-start | bytes 1572872 | tf_op jit(solution)/shard_map/ppermute | solution.py:109
  126.7 39.1 %collective-permute-start.25 = (bf16[2048,128]{0,1:T(8,128)(2,1)}, bf16[2048,128]{0,1:T(8,128)(2,1)}, u32[]{:S(2)}, u32[]{:S(2)}) collective-permute-start(bf16[2048,128]{0,1:T(8,128)(2,1)} %collective-permute-done.12), channel_id=1, source_target_pairs={{0,1},{1,0},{2,3},{3,2},{4,5},{5,4},{6,7},{7,6},{8,9},{9,8},{10,11... | collective-permute-start | bytes 1572872 | tf_op jit(solution)/shard_map/ppermute | solution.py:109
  137.8 41.8 %collective-permute-start.17 = (bf16[2048,256]{1,0:T(8,128)(2,1)}, bf16[2048,256]{1,0:T(8,128)(2,1)}, u32[]{:S(2)}, u32[]{:S(2)}) collective-permute-start(bf16[2048,256]{1,0:T(8,128)(2,1)} %constant_dynamic-update-slice_fusion), channel_id=1, source_target_pairs={{0,8},{8,0},{16,24},{24,16},{1,9},{9,1},{17,25},{25,17},{2,10},{10... | collective-permute-start | bytes 3145736 | tf_op jit(solution)/shard_map/ppermute | solution.py:109
  142.5 39.4 %collective-permute-start.19 = (bf16[2048,256]{1,0:T(8,128)(2,1)}, bf16[2048,256]{1,0:T(8,128)(2,1)}, u32[]{:S(2)}, u32[]{:S(2)}) collective-permute-start(bf16[2048,256]{1,0:T(8,128)(2,1)} %constant_dynamic-update-slice_fusion), channel_id=1, source_target_pairs={{0,16},{8,24},{16,0},{24,8},{1,17},{9,25},{17,1},{25,9},{2,18},{10... | collective-permute-start | bytes 3145736 | tf_op jit(solution)/shard_map/ppermute | solution.py:109
  149.1 35.2 %collective-permute-start.16 = (bf16[2048,256]{1,0:T(8,128)(2,1)}, bf16[2048,256]{1,0:T(8,128)(2,1)}, u32[]{:S(2)}, u32[]{:S(2)}) collective-permute-start(bf16[2048,256]{1,0:T(8,128)(2,1)} %constant_dynamic-update-slice_fusion), channel_id=1, source_target_pairs={{0,1},{1,0},{2,3},{3,2},{4,5},{5,4},{6,7},{7,6},{8,9},{9,8},{10,11... | collective-permute-start | bytes 3145736 | tf_op jit(solution)/shard_map/ppermute | solution.py:109
  179.3 223.1 %all-gather.6.cloned.1.call-start = ((), (), s32[]{:S(2)}) async-start(), calls=%async_computation.7 | async-start | bytes 9437184 | tf_op jit(solution)/shard_map/all_gather | solution.py:509
  196.7 27.5 %collective-permute-start.23 = (bf16[2048,256]{1,0:T(8,128)(2,1)S(1)}, bf16[2048,256]{1,0:T(8,128)(2,1)S(1)}, u32[]{:S(2)}, u32[]{:S(2)}) collective-permute-start(bf16[2048,256]{1,0:T(8,128)(2,1)S(1)} %constant_dynamic-update-slice_fusion.39), channel_id=1, source_target_pairs={{0,1},{1,0},{2,3},{3,2},{4,5},{5,4},{6,7},{7,6},{8,9},{9,8},{10,11... | collective-permute-start | bytes 3145736 | tf_op jit(solution)/shard_map/ppermute | solution.py:109
  196.8 25.6 %collective-permute-start.33 = (bf16[2048,256]{1,0:T(8,128)(2,1)S(1)}, bf16[2048,256]{1,0:T(8,128)(2,1)S(1)}, u32[]{:S(2)}, u32[]{:S(2)}) collective-permute-start(bf16[2048,256]{1,0:T(8,128)(2,1)S(1)} %copy-done.50), channel_id=1, source_target_pairs={{0,8},{8,0},{16,24},{24,16},{1,9},{9,1},{17,25},{25,17},{2,10},{10... | collective-permute-start | bytes 3145736 | tf_op jit(solution)/shard_map/ppermute | solution.py:109
  198.0 29.2 %collective-permute-start.35 = (bf16[2048,256]{1,0:T(8,128)(2,1)S(1)}, bf16[2048,256]{1,0:T(8,128)(2,1)}, u32[]{:S(2)}, u32[]{:S(2)}) collective-permute-start(bf16[2048,256]{1,0:T(8,128)(2,1)S(1)} %copy-done.50), channel_id=1, source_target_pairs={{0,16},{8,24},{16,0},{24,8},{1,17},{9,25},{17,1},{25,9},{2,18},{10... | collective-permute-start | bytes 3145736 | tf_op jit(solution)/shard_map/ppermute | solution.py:109
  199.1 32.0 %collective-permute-start.32 = (bf16[2048,256]{1,0:T(8,128)(2,1)S(1)}, bf16[2048,256]{1,0:T(8,128)(2,1)S(1)}, u32[]{:S(2)}, u32[]{:S(2)}) collective-permute-start(bf16[2048,256]{1,0:T(8,128)(2,1)S(1)} %copy-done.50), channel_id=1, source_target_pairs={{0,1},{1,0},{2,3},{3,2},{4,5},{5,4},{6,7},{7,6},{8,9},{9,8},{10,11... | collective-permute-start | bytes 3145736 | tf_op jit(solution)/shard_map/ppermute | solution.py:109
  292.2 250.9 %reduce-scatter.5.cloned.1.call-start = ((), (), s32[]{:S(2)}) async-start(), calls=%async_computation.8 | async-start | bytes 9437184 | tf_op jit(solution)/shard_map/reduce_scatter | solution.py:515
  294.1 70.5 %collective-permute-start.40 = (bf16[512,2048]{1,0:T(8,128)(2,1)S(1)}, bf16[512,2048]{1,0:T(8,128)(2,1)S(1)}, u32[]{:S(2)}, u32[]{:S(2)}) collective-permute-start(bf16[512,2048]{1,0:T(8,128)(2,1)S(1)} %pad_maximum_fusion.7), channel_id=1, source_target_pairs={{0,8},{8,0},{16,24},{24,16},{1,9},{9,1},{17,25},{25,17},{2,10},{10... | collective-permute-start | bytes 6291464 | tf_op jit(solution)/shard_map/ppermute | solution.py:109
  295.3 82.6 %collective-permute-start.41 = (bf16[512,2048]{1,0:T(8,128)(2,1)S(1)}, bf16[512,2048]{1,0:T(8,128)(2,1)S(1)}, u32[]{:S(2)}, u32[]{:S(2)}) collective-permute-start(bf16[512,2048]{1,0:T(8,128)(2,1)S(1)} %pad_maximum_fusion.7), channel_id=1, source_target_pairs={{0,16},{8,24},{16,0},{24,8},{1,17},{9,25},{17,1},{25,9},{2,18},{10... | collective-permute-start | bytes 6291464 | tf_op jit(solution)/shard_map/ppermute | solution.py:109
  296.3 64.8 %collective-permute-start.44 = (bf16[512,1024]{1,0:T(8,128)(2,1)S(1)}, bf16[512,1024]{1,0:T(8,128)(2,1)S(1)}, u32[]{:S(2)}, u32[]{:S(2)}) collective-permute-start(bf16[512,1024]{1,0:T(8,128)(2,1)S(1)} %copy-done.57), channel_id=1, source_target_pairs={{0,8},{8,0},{16,24},{24,16},{1,9},{9,1},{17,25},{25,17},{2,10},{10... | collective-permute-start | bytes 3145736 | tf_op jit(solution)/shard_map/ppermute | solution.py:109
  297.2 66.1 %collective-permute-start.45 = (bf16[512,1024]{1,0:T(8,128)(2,1)S(1)}, bf16[512,1024]{1,0:T(8,128)(2,1)S(1)}, u32[]{:S(2)}, u32[]{:S(2)}) collective-permute-start(bf16[512,1024]{1,0:T(8,128)(2,1)S(1)} %copy-done.57), channel_id=1, source_target_pairs={{0,16},{8,24},{16,0},{24,8},{1,17},{9,25},{17,1},{25,9},{2,18},{10... | collective-permute-start | bytes 3145736 | tf_op jit(solution)/shard_map/ppermute | solution.py:109
  364.7 33.5 %collective-permute-start.42 = (bf16[256,2048]{1,0:T(8,128)(2,1)S(1)}, bf16[256,2048]{1,0:T(8,128)(2,1)S(1)}, u32[]{:S(2)}, u32[]{:S(2)}) collective-permute-start(bf16[256,2048]{1,0:T(8,128)(2,1)S(1)} %slice.2166), channel_id=1, source_target_pairs={{0,16},{8,24},{16,0},{24,8},{1,17},{9,25},{17,1},{25,9},{2,18},{10... | collective-permute-start | bytes 3145736 | tf_op jit(solution)/shard_map/ppermute | solution.py:109
  442.5 195.9 %all-gather.8.cloned.1.call-start = ((), (), s32[]{:S(2)}) async-start(), calls=%async_computation.9 | async-start | bytes 9437184 | tf_op jit(solution)/shard_map/all_gather | solution.py:535
  557.8 278.7 %reduce-scatter.7.cloned.1.call-start = ((), (), s32[]{:S(2)}) async-start(), calls=%async_computation.10 | async-start | bytes 9437184 | tf_op jit(solution)/shard_map/reduce_scatter | solution.py:539
  685.8 354.5 %reduce-scatter.11.cloned.1.call-start = ((), (), s32[]{:S(2)}) async-start(), calls=%async_computation.12 | async-start | bytes 2949120 | tf_op jit(solution)/shard_map/reduce_scatter | solution.py:584
  725.1 40.1 %collective-permute-start.93 = (bf16[256,2048]{1,0:T(8,128)(2,1)S(1)}, bf16[256,2048]{1,0:T(8,128)(2,1)S(1)}, u32[]{:S(2)}, u32[]{:S(2)}) collective-permute-start(bf16[256,2048]{1,0:T(8,128)(2,1)S(1)} %get-tuple-element.300), channel_id=1, source_target_pairs={{0,8},{8,0},{16,24},{24,16},{1,9},{9,1},{17,25},{25,17},{2,10},{10... | collective-permute-start | bytes 3145736 | tf_op jit(solution)/shard_map/ppermute | solution.py:109
  726.5 39.4 %collective-permute-start.89 = (bf16[256,2048]{1,0:T(8,128)(2,1)S(1)}, bf16[256,2048]{1,0:T(8,128)(2,1)S(1)}, u32[]{:S(2)}, u32[]{:S(2)}) collective-permute-start(bf16[256,2048]{1,0:T(8,128)(2,1)S(1)} %get-tuple-element.302), channel_id=1, source_target_pairs={{0,16},{8,24},{16,0},{24,8},{1,17},{9,25},{17,1},{25,9},{2,18},{10... | collective-permute-start | bytes 3145736 | tf_op jit(solution)/shard_map/ppermute | solution.py:109
  745.3 69.7 %collective-permute-start.92 = (bf16[256,2048]{1,0:T(8,128)(2,1)}, bf16[256,2048]{1,0:T(8,128)(2,1)S(1)}, u32[]{:S(2)}, u32[]{:S(2)}) collective-permute-start(bf16[256,2048]{1,0:T(8,128)(2,1)} %get-tuple-element.299), channel_id=1, source_target_pairs={{0,8},{8,0},{16,24},{24,16},{1,9},{9,1},{17,25},{25,17},{2,10},{10... | collective-permute-start | bytes 3145736 | tf_op jit(solution)/shard_map/ppermute | solution.py:109
  762.7 52.8 %collective-permute-start.91 = (bf16[256,2048]{1,0:T(8,128)(2,1)S(1)}, bf16[256,2048]{1,0:T(8,128)(2,1)S(1)}, u32[]{:S(2)}, u32[]{:S(2)}) collective-permute-start(bf16[256,2048]{1,0:T(8,128)(2,1)S(1)} %get-tuple-element.301), channel_id=1, source_target_pairs={{0,16},{8,24},{16,0},{24,8},{1,17},{9,25},{17,1},{25,9},{2,18},{10... | collective-permute-start | bytes 3145736 | tf_op jit(solution)/shard_map/ppermute | solution.py:109
  764.2 34.1 %collective-permute-start.97 = (bf16[256,1024]{1,0:T(8,128)(2,1)S(1)}, bf16[256,1024]{1,0:T(8,128)(2,1)S(1)}, u32[]{:S(2)}, u32[]{:S(2)}) collective-permute-start(bf16[256,1024]{1,0:T(8,128)(2,1)S(1)} %get-tuple-element.310), channel_id=1, source_target_pairs={{0,16},{8,24},{16,0},{24,8},{1,17},{9,25},{17,1},{25,9},{2,18},{10... | collective-permute-start | bytes 1572872 | tf_op jit(solution)/shard_map/ppermute | solution.py:109
  765.2 34.5 %collective-permute-start.98 = (bf16[256,1024]{1,0:T(8,128)(2,1)S(1)}, bf16[256,1024]{1,0:T(8,128)(2,1)S(1)}, u32[]{:S(2)}, u32[]{:S(2)}) collective-permute-start(bf16[256,1024]{1,0:T(8,128)(2,1)S(1)} %get-tuple-element.309), channel_id=1, source_target_pairs={{0,8},{8,0},{16,24},{24,16},{1,9},{9,1},{17,25},{25,17},{2,10},{10... | collective-permute-start | bytes 1572872 | tf_op jit(solution)/shard_map/ppermute | solution.py:109
  765.8 40.7 %collective-permute-start.96 = (bf16[256,1024]{1,0:T(8,128)(2,1)S(1)}, bf16[256,1024]{1,0:T(8,128)(2,1)S(1)}, u32[]{:S(2)}, u32[]{:S(2)}) collective-permute-start(bf16[256,1024]{1,0:T(8,128)(2,1)S(1)} %get-tuple-element.305), channel_id=1, source_target_pairs={{0,8},{8,0},{16,24},{24,16},{1,9},{9,1},{17,25},{25,17},{2,10},{10... | collective-permute-start | bytes 1572872 | tf_op jit(solution)/shard_map/ppermute | solution.py:109
  799.7 33.3 %collective-permute-start.94 = (bf16[256,2048]{1,0:T(8,128)(2,1)S(1)}, bf16[256,2048]{1,0:T(8,128)(2,1)S(1)}, u32[]{:S(2)}, u32[]{:S(2)}) collective-permute-start(bf16[256,2048]{1,0:T(8,128)(2,1)S(1)} %get-tuple-element.303), channel_id=1, source_target_pairs={{0,16},{8,24},{16,0},{24,8},{1,17},{9,25},{17,1},{25,9},{2,18},{10... | collective-permute-start | bytes 3145736 | tf_op jit(solution)/shard_map/ppermute | solution.py:109
  806.5 26.4 %collective-permute-start.90 = (bf16[256,2048]{1,0:T(8,128)(2,1)S(1)}, bf16[256,2048]{1,0:T(8,128)(2,1)S(1)}, u32[]{:S(2)}, u32[]{:S(2)}) collective-permute-start(bf16[256,2048]{1,0:T(8,128)(2,1)S(1)} %get-tuple-element.304), channel_id=1, source_target_pairs={{0,8},{8,0},{16,24},{24,16},{1,9},{9,1},{17,25},{25,17},{2,10},{10... | collective-permute-start | bytes 3145736 | tf_op jit(solution)/shard_map/ppermute | solution.py:109
  813.1 103.3 %collective-permute-start.48 = (bf16[256,2048]{1,0:T(8,128)(2,1)}, bf16[256,2048]{1,0:T(8,128)(2,1)}, u32[]{:S(2)}, u32[]{:S(2)}) collective-permute-start(bf16[256,2048]{1,0:T(8,128)(2,1)} %get-tuple-element.351), channel_id=1, source_target_pairs={{0,1},{1,0},{2,3},{3,2},{4,5},{5,4},{6,7},{7,6},{8,9},{9,8},{10,11... | collective-permute-start | bytes 3145736 | tf_op jit(solution)/shard_map/ppermute | solution.py:109
  815.0 121.7 %collective-permute-start.76 = (bf16[256,1024]{1,0:T(8,128)(2,1)}, bf16[256,1024]{1,0:T(8,128)(2,1)}, u32[]{:S(2)}, u32[]{:S(2)}) collective-permute-start(bf16[256,1024]{1,0:T(8,128)(2,1)} %pad_maximum_fusion.33), channel_id=1, source_target_pairs={{0,1},{1,0},{2,3},{3,2},{4,5},{5,4},{6,7},{7,6},{8,9},{9,8},{10,11... | collective-permute-start | bytes 1572872 | tf_op jit(solution)/shard_map/ppermute | solution.py:109
  852.2 85.8 %collective-permute-start.75 = (bf16[256,2048]{1,0:T(8,128)(2,1)}, bf16[256,2048]{1,0:T(8,128)(2,1)}, u32[]{:S(2)}, u32[]{:S(2)}) collective-permute-start(bf16[256,2048]{1,0:T(8,128)(2,1)} %get-tuple-element.349), channel_id=1, source_target_pairs={{0,1},{1,0},{2,3},{3,2},{4,5},{5,4},{6,7},{7,6},{8,9},{9,8},{10,11... | collective-permute-start | bytes 3145736 | tf_op jit(solution)/shard_map/ppermute | solution.py:109
  876.3 178.1 %reduce-scatter.9.cloned.1.call-start = ((), (), s32[]{:S(2)}) async-start(), calls=%async_computation.11 | async-start | bytes 4718592 | tf_op jit(solution)/shard_map/reduce_scatter | solution.py:560
  942.6 71.6 %collective-permute-start.79 = (bf16[256,1024]{1,0:T(8,128)(2,1)S(1)}, bf16[256,1024]{1,0:T(8,128)(2,1)S(1)}, u32[]{:S(2)}, u32[]{:S(2)}) collective-permute-start(bf16[256,1024]{1,0:T(8,128)(2,1)S(1)} %get-tuple-element.320), channel_id=1, source_target_pairs={{0,16},{8,24},{16,0},{24,8},{1,17},{9,25},{17,1},{25,9},{2,18},{10... | collective-permute-start | bytes 1572872 | tf_op jit(solution)/shard_map/ppermute | solution.py:109
  945.4 33.7 %collective-permute-start.77 = (bf16[256,1024]{1,0:T(8,128)(2,1)S(1)}, bf16[256,1024]{1,0:T(8,128)(2,1)S(1)}, u32[]{:S(2)}, u32[]{:S(2)}) collective-permute-start(bf16[256,1024]{1,0:T(8,128)(2,1)S(1)} %get-tuple-element.317), channel_id=1, source_target_pairs={{0,16},{8,24},{16,0},{24,8},{1,17},{9,25},{17,1},{25,9},{2,18},{10... | collective-permute-start | bytes 1572872 | tf_op jit(solution)/shard_map/ppermute | solution.py:109
  947.1 44.6 %collective-permute-start.81 = (bf16[256,1024]{1,0:T(8,128)(2,1)S(1)}, bf16[256,1024]{1,0:T(8,128)(2,1)S(1)}, u32[]{:S(2)}, u32[]{:S(2)}) collective-permute-start(bf16[256,1024]{1,0:T(8,128)(2,1)S(1)} %get-tuple-element.318), channel_id=1, source_target_pairs={{0,8},{8,0},{16,24},{24,16},{1,9},{9,1},{17,25},{25,17},{2,10},{10... | collective-permute-start | bytes 1572872 | tf_op jit(solution)/shard_map/ppermute | solution.py:109
  958.3 55.9 %collective-permute-start.80 = (bf16[256,1024]{1,0:T(8,128)(2,1)S(1)}, bf16[256,1024]{1,0:T(8,128)(2,1)S(1)}, u32[]{:S(2)}, u32[]{:S(2)}) collective-permute-start(bf16[256,1024]{1,0:T(8,128)(2,1)S(1)} %get-tuple-element.319), channel_id=1, source_target_pairs={{0,8},{8,0},{16,24},{24,16},{1,9},{9,1},{17,25},{25,17},{2,10},{10... | collective-permute-start | bytes 1572872 | tf_op jit(solution)/shard_map/ppermute | solution.py:109
  958.9 41.6 %collective-permute-start.58 = (bf16[256,256]{1,0:T(8,128)(2,1)S(1)}, bf16[256,256]{1,0:T(8,128)(2,1)S(1)}, u32[]{:S(2)}, u32[]{:S(2)}) collective-permute-start(bf16[256,256]{1,0:T(8,128)(2,1)S(1)} %get-tuple-element.383), channel_id=1, source_target_pairs={{0,4},{1,5},{2,6},{3,7},{4,0},{5,1},{6,2},{7,3},{8,12},{9,13},{10,... | collective-permute-start | bytes 393224 | tf_op jit(solution)/shard_map/ppermute | solution.py:109
  (268 other events, 3723.3 us)
Sparse Core Ops, SparseCore 0:
  179.5 45.8 all-gather.3
  292.3 92.0 all-gather.5
  442.6 100.4 reduce-scatter.4
  557.9 80.4 all-gather.7
  685.9 88.0 reduce-scatter.6
  876.4 55.1 reduce-scatter.10
  933.9 51.9 reduce-scatter.8
